TPU v7x, 512 devices: a whole 4x4x16 slice. The times are simulated.
512 devices in a mesh: expert: 32 (over z, core), dp: 16 (over x, y).
Axes of the slice: x: 4, y: 4, z: 16, core: 2. Of those that a mesh axis runs over, the one named last changes fastest.
Arguments:
- patches: bfloat16 [16, 32, 128, 1664], P('dp', 'expert'), may hold values from -6 to 6
- grad_out: bfloat16 [16, 32, 128, 1664], P('dp', 'expert'), may hold values from -3 to 3
- weight_in: bfloat16 [32, 1664, 4096], P('expert', None, 'dp'), may hold values from -0.15625 to 0.15625
- weight_out: bfloat16 [32, 4096, 1664], P('expert', 'dp'), may hold values from -0.09375 to 0.09375
- gates: float32 [32, 16, 32], P('expert', 'dp'), may hold values from 0.1 to 1
- counts: int32 [16, 32, 32], P(None, None, 'expert'), may hold values from 0 to 2, as said below
- picks: int32 [16, 32, 32, 2], P('dp', 'expert'), may hold values from 0 to 127, as said below
Outputs:
- grad_patches: bfloat16 [16, 32, 128, 1664], P('dp', 'expert')
- grad_weight_in: bfloat16 [32, 1664, 4096], P('expert', None, 'dp')
- grad_weight_out: bfloat16 [32, 4096, 1664], P('expert', 'dp')
Inputs may be any that keep to these rules, and one draw needn't show every extreme that they name: For each group and expert the counts over the 32 owner blocks sum to exactly 32, and in every group each expert takes 2 patches from some owner block. `picks`: for each group, owner block and expert the entries are distinct; only the first counts[g, o, e] of them are taken, the rest are arbitrary patch indices of the block.
All inputs are finite; a program needn't handle non-finite values.
Results may differ from a plain program's by a relative error of at most 0.015.
Values may be sent and summed in bfloat16 or wider, within the bound.
A program may use at most 64 MiB of HBM per device.

v0:
```python
import jax
import jax.numpy as jnp
from jax import lax
from jax.sharding import PartitionSpec as P

gelu_scale = 0.7978845608028654
gelu_cubic = 0.044715


def gelu_parts(preact):
    inner_arg = gelu_scale * (preact + gelu_cubic * preact * preact * preact)
    tangent = jnp.tanh(inner_arg)
    gelu_value = 0.5 * preact * (1.0 + tangent)
    gelu_slope = 0.5 * (1.0 + tangent) + 0.5 * preact * (1.0 - tangent * tangent) * gelu_scale * (
        1.0 + 3.0 * gelu_cubic * preact * preact
    )
    return (gelu_value, gelu_slope)


def slot_tables(owner_counts, capacity):
    owners = owner_counts.shape[-1]
    slot_ends = jnp.cumsum(owner_counts, axis=-1)
    begins = slot_ends - owner_counts
    slot_ids = jnp.arange(capacity, dtype=jnp.int32)
    owner_of = jnp.sum((slot_ends[..., None, :] <= slot_ids[:, None]).astype(jnp.int32), axis=-1)
    matches = owner_of[..., None] == jnp.arange(owners, dtype=jnp.int32)
    rank_in = slot_ids - jnp.sum(jnp.where(matches, begins[..., None, :], 0), axis=-1)
    return (owner_of, rank_in)


def on_device(patches, grad_out, weight_in, weight_out, gates, counts, picks):
    tok_local = patches.shape[2]
    dim_model = patches.shape[3]
    experts = picks.shape[2]
    per_owner = picks.shape[3]
    groups = counts.shape[0]
    owners = counts.shape[1]
    capacity = gates.shape[2]
    local_in = weight_in[0]
    local_out = weight_out[0]
    chosen = picks[0, 0].reshape(experts * per_owner)
    send_in = jnp.take(patches[0, 0], chosen, axis=0).reshape(experts, per_owner, dim_model)
    send_grad = jnp.take(grad_out[0, 0], chosen, axis=0).reshape(experts, per_owner, dim_model)
    arrived_in, arrived_grad = (
        lax.all_to_all(send_in, "expert", split_axis=0, concat_axis=0, tiled=True),
        lax.all_to_all(send_grad, "expert", split_axis=0, concat_axis=0, tiled=True),
    )
    arrived_in = arrived_in.reshape(owners * per_owner, dim_model)
    arrived_grad = arrived_grad.reshape(owners * per_owner, dim_model)
    all_counts = counts[:, :, 0]
    group_index = lax.axis_index("dp")
    my_counts = lax.dynamic_index_in_dim(all_counts, group_index, 0, keepdims=False)
    my_begins = jnp.cumsum(my_counts) - my_counts
    rank_ids = jnp.arange(per_owner, dtype=jnp.int32)
    slot_of = (my_begins[:, None] + rank_ids[None, :]).reshape(owners * per_owner)
    is_valid = (rank_ids[None, :] < my_counts[:, None]).reshape(owners * per_owner)
    my_gates = gates[0, 0]
    slot_hits = (slot_of[:, None] == jnp.arange(capacity, dtype=jnp.int32)[None, :]) & is_valid[
        :, None
    ]
    padded_gates = jnp.sum(jnp.where(slot_hits, my_gates[None, :], 0.0), axis=1)
    scaled_rows = (padded_gates[:, None] * arrived_grad.astype(jnp.float32)).astype(jnp.bfloat16)
    piece_in = lax.all_gather(arrived_in, "dp", axis=0, tiled=True)
    piece_grad = lax.all_gather(scaled_rows, "dp", axis=0, tiled=True)
    preact = jnp.dot(piece_in, local_in, preferred_element_type=jnp.float32)
    gelu_value, gelu_slope = gelu_parts(preact)
    hidden = gelu_value.astype(jnp.bfloat16)
    grad_hidden = lax.dot_general(
        piece_grad, local_out, (((1,), (1,)), ((), ())), preferred_element_type=jnp.float32
    )
    grad_pre = (grad_hidden * gelu_slope).astype(jnp.bfloat16)
    sum_out = lax.dot_general(
        hidden, piece_grad, (((0,), (0,)), ((), ())), preferred_element_type=jnp.float32
    )
    sum_in = lax.dot_general(
        piece_in, grad_pre, (((0,), (0,)), ((), ())), preferred_element_type=jnp.float32
    )
    sum_in, sum_out, grad_stash = (sum_in, sum_out, grad_pre)
    owner_all, rank_all = slot_tables(all_counts, capacity)
    group_base = jnp.arange(groups, dtype=jnp.int32)[:, None] * (owners * per_owner)
    padded_index = (group_base + owner_all * per_owner + rank_all).reshape(groups * capacity)
    stash_rows = jnp.take(grad_stash, padded_index, axis=0)
    expert_grad = lax.psum_scatter(
        lax.dot_general(
            stash_rows, local_in, (((1,), (1,)), ((), ())), preferred_element_type=jnp.float32
        ).astype(jnp.bfloat16),
        "dp",
        scatter_dimension=0,
        tiled=True,
    )
    returned = jnp.take(expert_grad, jnp.clip(slot_of, 0, capacity - 1), axis=0)
    returned = jnp.where(is_valid[:, None], returned, jnp.zeros_like(returned))
    returned = returned.reshape(owners, per_owner, dim_model)
    arrived_back = lax.all_to_all(returned, "expert", split_axis=0, concat_axis=0, tiled=True)
    arrived_back = arrived_back.reshape(experts * per_owner, dim_model)
    owner_table = (jnp.arange(tok_local, dtype=jnp.int32)[:, None] == chosen[None, :]).astype(
        jnp.bfloat16
    )
    grad_local = jnp.dot(owner_table, arrived_back, preferred_element_type=jnp.float32).astype(
        jnp.bfloat16
    )
    return (
        grad_local[None, None],
        sum_in.astype(jnp.bfloat16)[None],
        sum_out.astype(jnp.bfloat16)[None],
    )


def solution(mesh):
    return jax.shard_map(
        on_device,
        mesh=mesh,
        in_specs=(
            P("dp", "expert", None, None),
            P("dp", "expert", None, None),
            P("expert", None, "dp"),
            P("expert", "dp", None),
            P("expert", "dp", None),
            P(None, None, "expert"),
            P("dp", "expert", None, None),
        ),
        out_specs=(P("dp", "expert", None, None), P("expert", None, "dp"), P("expert", "dp", None)),
        check_vma=False,
    )
```

profile of v0, /device:TPU:1, one launch (start us, length us, event | category | flops | bytes accessed | tf_op | source)
XLA Modules:
  0.0 311.9 jit_solution(8683857423019029709)
XLA Ops:
  7.2 0.0 copy-start
  7.2 0.0 all-gather.5.cloned.1.call-start
  7.2 0.8 copy.14
  8.1 0.1 eq.42
  8.2 0.0 copy-start.1
  8.2 0.0 copy-start.2
  8.2 2.0 gather_fusion.3
  10.2 2.0 gather_fusion.2
  12.2 0.1 broadcast_select_fusion.2
  12.3 0.1 reshape.235
  12.4 36.1 %all_to_all.15 = bf16[32,2,1664]{2,1,0:T(2,128)(2,1)S(1)} all-to-all(bf16[32,2,1664]{2,1,0:T(2,128)(2,1)S(1)} %reshape.235), channel_id=1, replica_groups=mesh['expert'=32,'dp'=16] {'expert'}, dimensions={0} | all-to-all | bytes 425984 | tf_op jit(solution)/shard_map/all_to_all | solution.py:45
  48.6 0.8 reshape.236
  49.3 0.0 all-gather.5.cloned.1.call-update
  49.3 0.8 reshape.234
  50.1 4.9 %all-to-all-start = ((bf16[32,2,1664]{2,1,0:T(2,128)(2,1)}), bf16[32,2,1664]{2,1,0:T(2,128)(2,1)S(1)}, u32[]{:S(2)}, u32[]{:S(2)}) async-start(bf16[32,2,1664]{2,1,0:T(2,128)(2,1)} %reshape.234), calls=%async_computation | async-start | bytes 425984 | tf_op jit(solution)/shard_map/all_to_all | solution.py:46
  55.0 0.0 all-gather.3.cloned.1.call-start
  55.0 0.0 copy-done.1
  55.1 0.1 copy.15
  55.2 0.1 reduce-window.8
  55.2 0.1 reduce
  55.3 0.1 iota_compare_fusion.5
  55.4 0.1 lt.83
  55.5 0.1 broadcast_clamp_fusion
  55.6 0.1 add.147
  55.7 0.0 copy-done.2
  55.7 0.1 select_reduce_fusion.1
  55.8 18.8 %all-to-all-done = bf16[32,2,1664]{2,1,0:T(2,128)(2,1)S(1)} async-done(((bf16[32,2,1664]{2,1,0:T(2,128)(2,1)}), bf16[32,2,1664]{2,1,0:T(2,128)(2,1)S(1)}, u32[]{:S(2)}, u32[]{:S(2)}) %all-to-all-start) | async-done | bytes 213024 | tf_op jit(solution)/shard_map/all_to_all | solution.py:46
  74.6 0.1 reshape.238
  74.7 0.8 multiply_convert_fusion.2
  75.5 0.0 all-gather.3.cloned.1.call-update
  75.5 0.0 reduce-scatter.2.cloned.1.call-start
  75.5 0.2 reduce_window_sum.18
  75.7 0.3 convert_reduce_fusion
  76.1 0.5 select_reduce_fusion
  76.5 0.1 subtract_add_fusion
  76.6 0.1 add.152
  76.7 0.1 add.144
  76.8 0.0 copy-start.4
  76.8 28.1 %all-gather.5.cloned.1.call-done = bf16[1024,1664]{1,0:T(8,128)(2,1)} async-done(((bf16[64,1664]{1,0:T(8,128)(2,1)}), bf16[1024,1664]{1,0:T(8,128)(2,1)}) %all-gather.5.cloned.1.call-update) | async-done | bytes 3407888 | tf_op jit(solution)/shard_map/all_gather | solution.py:63
  104.9 0.0 copy-done
  104.9 3.1 fusion.10
  108.0 63.5 %all-gather.3.cloned.1.call-done = bf16[1024,1664]{1,0:T(8,128)(2,1)} async-done(((bf16[64,1664]{1,0:T(8,128)(2,1)}), bf16[1024,1664]{1,0:T(8,128)(2,1)}) %all-gather.3.cloned.1.call-update) | async-done | bytes 3407888 | tf_op jit(solution)/shard_map/all_gather | solution.py:64
  171.5 0.0 copy-done.4
  171.5 3.5 %fusion.3 = bf16[1024,256]{1,0:T(8,128)(2,1)S(1)} fusion(bf16[1024,1664]{1,0:T(8,128)(2,1)} %all-gather.3.cloned.1.call-done, f32[1024,256]{1,0:T(8,128)S(1)} %fusion.10, bf16[1,256,1664]{2,1,0:T(8,128)(2,1)S(1)} %copy-done.4), kind=kOutput, calls=%fused_computation.14 | convolution fusion | flops 877395968 | bytes 5832704 | tf_op jit(solution)/shard_map/dot_general | solution.py:68
  174.9 2.0 gather_fusion
  176.9 1.9 convolution_convert_fusion
  178.8 0.0 reduce-scatter.2.cloned.1.call-update
  178.8 0.1 min.12
  179.0 0.1 compare_and_fusion
  179.0 87.9 %reduce-scatter.2.cloned.1.call-done = bf16[32,1664]{1,0:T(8,128)(2,1)} async-done(((bf16[512,1664]{1,0:T(8,128)(2,1)}), bf16[32,1664]{1,0:T(8,128)(2,1)}) %reduce-scatter.2.cloned.1.call-update) | async-done | bytes 106512 | tf_op jit(solution)/shard_map/reduce_scatter | solution.py:83
  267.0 1.8 gather_fusion.1
  268.8 0.1 gather.15
  268.9 1.1 broadcast_select_fusion.1
  270.0 14.7 %all-to-all-start.2 = ((bf16[32,2,1664]{2,1,0:T(2,128)(2,1)}), bf16[32,2,1664]{2,1,0:T(2,128)(2,1)S(1)}, u32[]{:S(2)}, u32[]{:S(2)}) async-start(bf16[32,2,1664]{2,1,0:T(2,128)(2,1)} %broadcast_select_fusion.1), calls=%async_computation.3 | async-start | bytes 425984 | tf_op jit(solution)/shard_map/all_to_all | solution.py:94
  284.7 0.0 copy-start.3
  284.7 4.1 %fusion = bf16[1,1664,256]{2,1,0:T(8,128)(2,1)} fusion(bf16[1024,1664]{1,0:T(8,128)(2,1)} %all-gather.5.cloned.1.call-done, bf16[1024,256]{1,0:T(8,128)(2,1)S(1)} %fusion.3), kind=kOutput, calls=%fused_computation.7 | convolution fusion | flops 872841216 | bytes 4784128 | tf_op jit(solution)/shard_map/dot_general | solution.py:75
  288.8 0.0 copy-done.3
  288.8 2.1 fusion.1
  290.9 13.3 %all-to-all-done.2 = bf16[32,2,1664]{2,1,0:T(2,128)(2,1)S(1)} async-done(((bf16[32,2,1664]{2,1,0:T(2,128)(2,1)}), bf16[32,2,1664]{2,1,0:T(2,128)(2,1)S(1)}, u32[]{:S(2)}, u32[]{:S(2)}) %all-to-all-start.2) | async-done | bytes 213024 | tf_op jit(solution)/shard_map/all_to_all | solution.py:94
  304.2 0.1 reshape.237
  304.3 1.0 fusion.2
  (12 shorter events, 0.1 us)
Async XLA Ops:
  7.2 97.7 %copy-start = (bf16[1,1664,256]{2,1,0:T(8,128)(2,1)S(1)}, bf16[1,1664,256]{2,1,0:T(8,128)(2,1)}, u32[]{:S(2)}) copy-start(bf16[1,1664,256]{2,1,0:T(8,128)(2,1)} %param.11) | copy-start | bytes 2555908
  7.2 97.7 %all-gather.5.cloned.1.call-start = ((), (), s32[]{:S(2)}) async-start(), calls=%async_computation.5 | async-start | bytes 3620864 | tf_op jit(solution)/shard_map/all_gather | solution.py:63
  8.2 46.8 %copy-start.1 = (s32[16,32,1]{1,2,0:T(1,128)S(1)}, s32[16,32,1]{1,2,0:T(1,128)}, u32[]{:S(2)}) copy-start(s32[16,32,1]{1,2,0:T(1,128)} %param.14) | copy-start | bytes 6148
  8.2 47.5 %copy-start.2 = (f32[1,1,32]{2,1,0:T(1,128)S(1)}, f32[1,1,32]{2,1,0:T(1,128)}, u32[]{:S(2)}) copy-start(f32[1,1,32]{2,1,0:T(1,128)} %param.13) | copy-start | bytes 388
  50.1 24.5 %all-to-all-start = ((bf16[32,2,1664]{2,1,0:T(2,128)(2,1)}), bf16[32,2,1664]{2,1,0:T(2,128)(2,1)S(1)}, u32[]{:S(2)}, u32[]{:S(2)}) async-start(bf16[32,2,1664]{2,1,0:T(2,128)(2,1)} %reshape.234), calls=%async_computation | async-start | bytes 425984 | tf_op jit(solution)/shard_map/all_to_all | solution.py:46
  55.0 116.5 %all-gather.3.cloned.1.call-start = ((), (), s32[]{:S(2)}) async-start(), calls=%async_computation.4 | async-start | bytes 3620864 | tf_op jit(solution)/shard_map/all_gather | solution.py:64
  75.5 191.5 %reduce-scatter.2.cloned.1.call-start = ((), (), s32[]{:S(2)}) async-start(), calls=%async_computation.6 | async-start | bytes 1810432 | tf_op jit(solution)/shard_map/reduce_scatter | solution.py:83
  76.8 94.6 %copy-start.4 = (bf16[1,256,1664]{2,1,0:T(8,128)(2,1)S(1)}, bf16[1,256,1664]{2,1,0:T(8,128)(2,1)}, u32[]{:S(2)}) copy-start(bf16[1,256,1664]{2,1,0:T(8,128)(2,1)} %param.12) | copy-start | bytes 2555908
  270.0 34.3 %all-to-all-start.2 = ((bf16[32,2,1664]{2,1,0:T(2,128)(2,1)}), bf16[32,2,1664]{2,1,0:T(2,128)(2,1)S(1)}, u32[]{:S(2)}, u32[]{:S(2)}) async-start(bf16[32,2,1664]{2,1,0:T(2,128)(2,1)} %broadcast_select_fusion.1), calls=%async_computation.3 | async-start | bytes 425984 | tf_op jit(solution)/shard_map/all_to_all | solution.py:94
  284.7 4.1 %copy-start.3 = (bf16[1024,1664]{1,0:T(8,128)(2,1)S(1)}, bf16[1024,1664]{1,0:T(8,128)(2,1)}, u32[]{:S(2)}) copy-start(bf16[1024,1664]{1,0:T(8,128)(2,1)} %all-gather.3.cloned.1.call-done) | copy-start | bytes 10223620
Sparse Core Ops, SparseCore 0:
  49.5 55.3 all-gather.4
  108.5 62.8 all-gather.2
  179.0 87.9 reduce-scatter.1
where the time goes:
time: 312 us
  waiting for transfers between devices  212 us (68%)
  blocking collectives  36.1 us (12%)
  starting transfers between devices  19.7 us (6%)
  matrix products  15.7 us (5%)
  between operations  14 us (4%)
  local copies, waits for them, and re-layouts  11.2 us (4%)
  other arithmetic  3.6 us (1%)
    reduce_scatter x1, waiting for transfers between devices, on_device(): lax.psum_scatter(lax.dot_general(stash_rows, local_in, (((1,), (1,)), (()...  87.9 us
    all_gather x1, waiting for transfers between devices, on_device(): piece_grad = lax.all_gather(scaled_rows, 'dp', axis=0, tiled=True)  63.5 us
    all_to_all x1, blocking collectives, on_device(): lax.all_to_all(send_in, 'expert', split_axis=0, concat_axis=0, tiled=True)  36.1 us
    all_gather x1, waiting for transfers between devices, on_device(): piece_in = lax.all_gather(arrived_in, 'dp', axis=0, tiled=True)  28.1 us
    all_to_all x1, waiting for transfers between devices, on_device(): lax.all_to_all(send_grad, 'expert', split_axis=0, concat_axis=0, tiled=True)  18.8 us
    all_to_all x1, starting transfers between devices, on_device(): lax.all_to_all(returned, 'expert', split_axis=0, concat_axis=0, tiled=True)  14.7 us
    all_to_all x1, waiting for transfers between devices, on_device(): lax.all_to_all(returned, 'expert', split_axis=0, concat_axis=0, tiled=True)  13.3 us
  transfers between devices with their start and end apart: 5, of which 5 were waited for; matrix products, arithmetic and copies ran while one was open for 4% of the time, Pallas kernels for 0%

commit v1 on v0

v1 whole, which is shorter than its diff:
```python
import functools

import jax
import jax.numpy as jnp
from jax import lax
from jax.experimental import pallas as pl
from jax.experimental.pallas import tpu as pltpu
from jax.sharding import PartitionSpec as P

MESH = pl.DeviceIdType.MESH
SIDE = 4
HALF = 16

gelu_scale = 0.7978845608028654
gelu_cubic = 0.044715


def gelu_parts(preact):
    inner_arg = gelu_scale * (preact + gelu_cubic * preact * preact * preact)
    tangent = jnp.tanh(inner_arg)
    gelu_value = 0.5 * preact * (1.0 + tangent)
    gelu_slope = 0.5 * (1.0 + tangent) + 0.5 * preact * (1.0 - tangent * tangent) * gelu_scale * (
        1.0 + 3.0 * gelu_cubic * preact * preact
    )
    return (gelu_value, gelu_slope)


def meet(axis, peers):
    barrier = pltpu.get_barrier_semaphore()
    for peer in peers:
        pl.semaphore_signal(barrier, inc=1, device_id={axis: peer}, device_id_type=MESH)
    pl.semaphore_wait(barrier, len(peers))


def exchange_kernel(count, size, *refs):
    sources, targets = refs[:count], refs[count : 2 * count]
    send_sem, recv_sem, own_sem = refs[2 * count :]
    me = lax.axis_index("expert")
    barrier = pltpu.get_barrier_semaphore()

    def offset_of(step):
        sign = 1 - 2 * lax.rem(step, 2)
        return size // 2 + sign * lax.div(step + 1, 2)

    def greet(step, carry):
        peer = lax.rem(me + offset_of(step), size)
        pl.semaphore_signal(barrier, inc=1, device_id={"expert": peer}, device_id_type=MESH)
        return carry

    lax.fori_loop(0, size - 1, greet, 0)
    own = [
        pltpu.make_async_copy(sources[i].at[me], targets[i].at[me], own_sem.at[i])
        for i in range(count)
    ]
    for copy in own:
        copy.start()
    pl.semaphore_wait(barrier, size - 1)

    def outgoing(i, step):
        offset = offset_of(step)
        peer = lax.rem(me + offset, size)
        return pltpu.make_async_remote_copy(
            src_ref=sources[i].at[peer],
            dst_ref=targets[i].at[me],
            send_sem=send_sem.at[i, offset],
            recv_sem=recv_sem.at[i, offset],
            device_id={"expert": peer},
            device_id_type=MESH,
        )

    def incoming(i, step):
        offset = offset_of(step)
        peer = lax.rem(me + size - offset, size)
        return pltpu.make_async_remote_copy(
            src_ref=sources[i].at[peer],
            dst_ref=targets[i].at[peer],
            send_sem=send_sem.at[i, offset],
            recv_sem=recv_sem.at[i, offset],
            device_id={"expert": peer},
            device_id_type=MESH,
        )

    for i in range(count):

        def launch(step, carry, i=i):
            outgoing(i, step).start()
            return carry

        lax.fori_loop(0, size - 1, launch, 0)
    for i in range(count):

        def finish(step, carry, i=i):
            incoming(i, step).wait_recv()
            outgoing(i, step).wait_send()
            return carry

        lax.fori_loop(0, size - 1, finish, 0)
    for copy in own:
        copy.wait()


def exchange(collective_id, *arrays):
    size = arrays[0].shape[0]
    count = len(arrays)
    in_vmem = pl.BlockSpec(memory_space=pltpu.VMEM)
    return pl.pallas_call(
        functools.partial(exchange_kernel, count, size),
        out_shape=[jax.ShapeDtypeStruct(a.shape, a.dtype) for a in arrays],
        in_specs=[in_vmem] * count,
        out_specs=[in_vmem] * count,
        scratch_shapes=[
            pltpu.SemaphoreType.DMA((count, size)),
            pltpu.SemaphoreType.DMA((count, size)),
            pltpu.SemaphoreType.DMA((count,)),
        ],
        compiler_params=pltpu.CompilerParams(collective_id=collective_id, has_side_effects=True),
    )(*arrays)


def wrap(value):
    return lax.rem(value + 2 * SIDE, SIDE)


def place(half, first, second):
    return first * SIDE + second if half == 0 else second * SIDE + first


def spread_kernel(in_ref, grad_ref, in_all, grad_all, send_sem, recv_sem, own_sem):
    me = lax.axis_index("dp")
    spot_x, spot_y = lax.div(me, SIDE), lax.rem(me, SIDE)
    inputs, outputs = (in_ref, grad_ref), (in_all, grad_all)
    own = [pltpu.make_async_copy(inputs[i], outputs[i].at[me], own_sem.at[i]) for i in range(2)]
    for copy in own:
        copy.start()
    meet(
        "dp",
        [
            place(0, wrap(spot_x + 1), spot_y),
            place(0, wrap(spot_x - 1), spot_y),
            place(0, spot_x, wrap(spot_y + 1)),
            place(0, spot_x, wrap(spot_y - 1)),
        ],
    )
    shifts = (0, -1, 1, 2)
    moves = ((0, 1), (1, 1), (0, -1), (1, -1), (0, 1), (1, -1))

    def piece(half, stage, move, incoming):
        which, way = moves[move]
        first, second = (spot_x, spot_y) if half == 0 else (spot_y, spot_x)
        rows = pl.ds(half * HALF, HALF)
        back = (0 if move < 4 else -way) - (way if incoming else 0)
        if stage == 0:
            block = place(half, wrap(first + back), second)
            peer = place(half, wrap(first + way), second)
        else:
            held = wrap(first + shifts[stage - 1])
            block = place(half, held, wrap(second + back))
            peer = place(half, first, wrap(second + way))
        target = outputs[which].at[block, rows, :]
        source = target
        if not incoming and move < 4 and stage < 2:
            source = inputs[which].at[rows, :]
        return pltpu.make_async_remote_copy(
            src_ref=source,
            dst_ref=target,
            send_sem=send_sem.at[half, stage, move],
            recv_sem=recv_sem.at[half, stage, move],
            device_id={"dp": peer},
            device_id_type=MESH,
        )

    def launch(half, stage, move):
        piece(half, stage, move, False).start()

    def arrive(half, stage, move):
        piece(half, stage, move, True).wait_recv()

    def relay(half, stage):
        arrive(half, stage, 0)
        launch(half, stage, 4)
        arrive(half, stage, 3)
        launch(half, stage, 5)

    halves = range(2)
    for stage in (0, 1):
        for move in range(4):
            for half in halves:
                launch(half, stage, move)
    for half in halves:
        relay(half, 0)
    for half in halves:
        arrive(half, 0, 1)
        for move in range(4):
            launch(half, 2, move)
    for half in halves:
        arrive(half, 0, 2)
        for move in range(4):
            launch(half, 3, move)
    for half in halves:
        relay(half, 1)
    for half in halves:
        arrive(half, 0, 4)
        arrive(half, 0, 5)
        for move in range(4):
            launch(half, 4, move)
    for stage in (2, 3, 4):
        for half in halves:
            relay(half, stage)
    for stage in (1, 2, 3, 4):
        for half in halves:
            for move in (1, 2, 4, 5):
                arrive(half, stage, move)
    for stage in range(5):
        for half in halves:
            for move in range(6):
                piece(half, stage, move, False).wait_send()
    for copy in own:
        copy.wait()


def spread(collective_id, rows_in, rows_grad):
    in_vmem = pl.BlockSpec(memory_space=pltpu.VMEM)
    whole = jax.ShapeDtypeStruct((SIDE * SIDE,) + rows_in.shape, rows_in.dtype)
    return pl.pallas_call(
        spread_kernel,
        out_shape=[whole, whole],
        in_specs=[in_vmem] * 2,
        out_specs=[in_vmem] * 2,
        scratch_shapes=[
            pltpu.SemaphoreType.DMA((2, 5, 6)),
            pltpu.SemaphoreType.DMA((2, 5, 6)),
            pltpu.SemaphoreType.DMA((2,)),
        ],
        compiler_params=pltpu.CompilerParams(collective_id=collective_id, has_side_effects=True),
    )(rows_in, rows_grad)


def collect_kernel(parts, total, near, passing, summed, last, send_sem, recv_sem):
    me = lax.axis_index("dp")
    spot_x, spot_y = lax.div(me, SIDE), lax.rem(me, SIDE)
    meet(
        "dp",
        [place(0, wrap(spot_x + shift), spot_y) for shift in (1, -1, 2)]
        + [place(0, spot_x, wrap(spot_y + shift)) for shift in (1, -1, 2)],
    )

    def unit(half, spot, begin=0, count=SIDE):
        rows = pl.ds(half * HALF, HALF)
        if half == 0:
            return parts.at[spot, pl.ds(begin, count), rows, :]
        return parts.at[pl.ds(begin, count), spot, rows, :]

    def piece(half, move):
        first, second = (spot_x, spot_y) if half == 0 else (spot_y, spot_x)
        if move == 0:
            way, source, target = 1, unit(half, wrap(first + 1)), near.at[half, 0]
        elif move == 1:
            way, source, target = -1, unit(half, wrap(first - 1)), near.at[half, 1]
        elif move == 2:
            way, source, target = 1, unit(half, wrap(first + 2), 0, 2), passing.at[half, 0]
        elif move == 3:
            way, source, target = -1, unit(half, wrap(first + 2), 2, 2), passing.at[half, 1]
        elif move == 4:
            way, source, target = 1, passing.at[half, 0], near.at[half, 2, pl.ds(0, 2)]
        elif move == 5:
            way, source, target = -1, passing.at[half, 1], near.at[half, 2, pl.ds(2, 2)]
        else:
            way = (1, -1, 2)[move - 6]
            source, target = summed.at[half, wrap(second + way)], last.at[half, move - 6]
        if move < 6:
            peer = place(half, wrap(first + way), second)
        else:
            peer = place(half, first, wrap(second + way))
        return pltpu.make_async_remote_copy(
            src_ref=source,
            dst_ref=target,
            send_sem=send_sem.at[half, move],
            recv_sem=recv_sem.at[half, move],
            device_id={"dp": peer},
            device_id_type=MESH,
        )

    halves = range(2)
    for move in (2, 3, 0, 1):
        for half in halves:
            piece(half, move).start()
    for half in halves:
        piece(half, 2).wait_recv()
        piece(half, 4).start()
        piece(half, 3).wait_recv()
        piece(half, 5).start()
    for half in halves:
        for move in (0, 1, 4, 5):
            piece(half, move).wait_recv()
        mine = spot_x if half == 0 else spot_y
        for spot in range(SIDE):
            rows = slice(half * HALF, half * HALF + HALF)
            own = parts[mine, spot, rows, :] if half == 0 else parts[spot, mine, rows, :]
            value = own.astype(jnp.float32)
            for source in range(3):
                value = value + near[half, source, spot].astype(jnp.float32)
            summed[half, spot] = value.astype(summed.dtype)
        for move in (8, 6, 7):
            piece(half, move).start()
    for half in halves:
        for move in (6, 7, 8):
            piece(half, move).wait_recv()
        mine = spot_y if half == 0 else spot_x
        value = summed[half, mine].astype(jnp.float32)
        for source in range(3):
            value = value + last[half, source].astype(jnp.float32)
        total[half * HALF : half * HALF + HALF, :] = value.astype(total.dtype)
    for half in halves:
        for move in range(9):
            piece(half, move).wait_send()


def collect(collective_id, parts):
    rows, width = parts.shape[2:]
    in_vmem = pl.BlockSpec(memory_space=pltpu.VMEM)
    kind = parts.dtype
    return pl.pallas_call(
        collect_kernel,
        out_shape=jax.ShapeDtypeStruct((rows, width), kind),
        in_specs=[in_vmem],
        out_specs=in_vmem,
        scratch_shapes=[
            pltpu.VMEM((2, 3, SIDE, HALF, width), kind),
            pltpu.VMEM((2, 2, 2, HALF, width), kind),
            pltpu.VMEM((2, SIDE, HALF, width), kind),
            pltpu.VMEM((2, 3, HALF, width), kind),
            pltpu.SemaphoreType.DMA((2, 9)),
            pltpu.SemaphoreType.DMA((2, 9)),
        ],
        compiler_params=pltpu.CompilerParams(collective_id=collective_id, has_side_effects=True),
    )(parts)


def on_device(patches, grad_out, weight_in, weight_out, gates, counts, picks):
    tok_local = patches.shape[2]
    dim_model = patches.shape[3]
    experts = picks.shape[2]
    per_owner = picks.shape[3]
    groups = counts.shape[0]
    owners = counts.shape[1]
    capacity = gates.shape[2]
    local_in = weight_in[0]
    local_out = weight_out[0]
    chosen = picks[0, 0].reshape(experts * per_owner)
    send_in = jnp.take(patches[0, 0], chosen, axis=0).reshape(experts, per_owner, dim_model)
    send_grad = jnp.take(grad_out[0, 0], chosen, axis=0).reshape(experts, per_owner, dim_model)
    arrived_in, arrived_grad = exchange(1, send_in, send_grad)
    arrived_in = arrived_in.reshape(owners * per_owner, dim_model)
    arrived_grad = arrived_grad.reshape(owners * per_owner, dim_model)
    group_index = lax.axis_index("dp")
    my_counts = lax.dynamic_index_in_dim(counts[:, :, 0], group_index, 0, keepdims=False)
    my_begins = jnp.cumsum(my_counts) - my_counts
    rank_ids = jnp.arange(per_owner, dtype=jnp.int32)
    slot_of = (my_begins[:, None] + rank_ids[None, :]).reshape(owners * per_owner)
    is_valid = (rank_ids[None, :] < my_counts[:, None]).reshape(owners * per_owner)
    slot_hits = (slot_of[:, None] == jnp.arange(capacity, dtype=jnp.int32)[None, :]) & is_valid[
        :, None
    ]
    slot_hits = slot_hits.astype(jnp.bfloat16)
    rows_in = lax.dot_general(
        slot_hits, arrived_in, (((0,), (0,)), ((), ())), preferred_element_type=jnp.float32
    ).astype(jnp.bfloat16)
    rows_grad = lax.dot_general(
        slot_hits, arrived_grad, (((0,), (0,)), ((), ())), preferred_element_type=jnp.float32
    )
    scaled_rows = (gates[0, 0][:, None] * rows_grad).astype(jnp.bfloat16)
    piece_in, piece_grad = spread(2, rows_in, scaled_rows)
    piece_in = piece_in.reshape(groups * capacity, dim_model)
    piece_grad = piece_grad.reshape(groups * capacity, dim_model)
    preact = jnp.dot(piece_in, local_in, preferred_element_type=jnp.float32)
    gelu_value, gelu_slope = gelu_parts(preact)
    hidden = gelu_value.astype(jnp.bfloat16)
    grad_hidden = lax.dot_general(
        piece_grad, local_out, (((1,), (1,)), ((), ())), preferred_element_type=jnp.float32
    )
    grad_pre = (grad_hidden * gelu_slope).astype(jnp.bfloat16)
    partial = lax.dot_general(
        grad_pre, local_in, (((1,), (1,)), ((), ())), preferred_element_type=jnp.float32
    ).astype(jnp.bfloat16)
    expert_grad = collect(3, partial.reshape(SIDE, SIDE, capacity, dim_model))
    sum_out = lax.dot_general(
        hidden, piece_grad, (((0,), (0,)), ((), ())), preferred_element_type=jnp.float32
    )
    sum_in = lax.dot_general(
        piece_in, grad_pre, (((0,), (0,)), ((), ())), preferred_element_type=jnp.float32
    )
    returned = jnp.dot(slot_hits, expert_grad, preferred_element_type=jnp.float32).astype(
        jnp.bfloat16
    )
    (arrived_back,) = exchange(4, returned.reshape(owners, per_owner, dim_model))
    arrived_back = arrived_back.reshape(experts * per_owner, dim_model)
    owner_table = (jnp.arange(tok_local, dtype=jnp.int32)[:, None] == chosen[None, :]).astype(
        jnp.bfloat16
    )
    grad_local = jnp.dot(owner_table, arrived_back, preferred_element_type=jnp.float32).astype(
        jnp.bfloat16
    )
    return (
        grad_local[None, None],
        sum_in.astype(jnp.bfloat16)[None],
        sum_out.astype(jnp.bfloat16)[None],
    )


def solution(mesh):
    return jax.shard_map(
        on_device,
        mesh=mesh,
        in_specs=(
            P("dp", "expert", None, None),
            P("dp", "expert", None, None),
            P("expert", None, "dp"),
            P("expert", "dp", None),
            P("expert", "dp", None),
            P(None, None, "expert"),
            P("dp", "expert", None, None),
        ),
        out_specs=(P("dp", "expert", None, None), P("expert", None, "dp"), P("expert", "dp", None)),
        check_vma=False,
    )
```

time: 312 us -> 134 us (0.43)
  waiting for transfers between devices: 212 us -> 0 us
  Pallas kernels: 0 us -> 109 us
  blocking collectives: 36.1 us -> 0 us
  starting transfers between devices: 19.7 us -> 0 us
  between operations: 14 us -> 0.83 us
  matrix products: 15.7 us -> 12.2 us
    pallas_call x0 -> x4, Pallas kernels: none -> 109 us  [the longest x2 64 us: exchange(): pl.pallas_call(functools.partial(exchange_kernel, count, size), out_shape...]
    all_gather x2 -> x0, waiting for transfers between devices: 91.5 us -> none  [the longest x1 63.5 us: on_device(): piece_grad = lax.all_gather(scaled_rows, 'dp', axis=0, tiled=True)]
    reduce_scatter x1 -> x0, waiting for transfers between devices: 87.9 us -> none  [on_device(): lax.psum_scatter(lax.dot_general(stash_rows, local_in, (((1,), (1,)), (()...]
    all_to_all x1 -> x0, blocking collectives: 36.1 us -> none  [on_device(): lax.all_to_all(send_in, 'expert', split_axis=0, concat_axis=0, tiled=True)]
    all_to_all x2 -> x0, waiting for transfers between devices: 32.1 us -> none  [the longest x1 18.8 us: on_device(): lax.all_to_all(send_grad, 'expert', split_axis=0, concat_axis=0, tiled=True)]
    all_to_all x2 -> x0, starting transfers between devices: 19.5 us -> none  [the longest x1 14.7 us: on_device(): lax.all_to_all(returned, 'expert', split_axis=0, concat_axis=0, tiled=True)]
    gather x3 -> x0, local copies, waits for them, and re-layouts: 3.87 us -> none  [the longest x1 1.95 us: on_device(): stash_rows = jnp.take(grad_stash, padded_index, axis=0)]
  transfers between devices with their start and end apart: 5 -> 0, of which waited for: 5 -> 0; matrix products, arithmetic and copies ran while one was open for 4% -> 0% of each run, Pallas kernels for 0% -> 0%
where the time goes in v1:
time: 134 us; the launch traced here: 133 us
  Pallas kernels  109 us (81%)
  matrix products  12.2 us (9%)
  local copies, waits for them, and re-layouts  10.1 us (8%)
    pallas_call x2, Pallas kernels, exchange(): pl.pallas_call(functools.partial(exchange_kernel, count, size), out_shape...  64 us
    pallas_call x1, Pallas kernels, spread(): pl.pallas_call(spread_kernel, out_shape=[whole, whole], in_specs=[in_vmem...  27.8 us
    pallas_call x1, Pallas kernels, collect(): pl.pallas_call(collect_kernel, out_shape=jax.ShapeDtypeStruct((rows, widt...  17.4 us

profile of v1, /device:TPU:1, one launch (start us, length us, event | category | flops | bytes accessed | tf_op | source)
XLA Modules:
  0.0 133.3 jit_solution(8813980375213449784)
XLA Ops:
  0.6 0.0 copy-start
  0.6 0.0 copy-start.1
  0.7 0.8 fusion.30
  1.4 0.1 copy.13
  1.5 0.1 reduce-window.8
  1.6 0.1 reduce
  1.7 0.7 fusion.35
  2.3 0.1 iota_compare_fusion.3
  2.4 0.1 lt.31
  2.5 0.1 iota_add_fusion
  2.6 0.1 add.49
  2.7 0.8 copy.12
  3.5 0.1 eq.29
  3.6 2.0 %gather_fusion.1 = bf16[64,1664]{1,0:T(8,128)(2,1)S(1)} fusion(bf16[128,1664]{1,0:T(8,128)(2,1)} %bitcast.38, s32[1024]{0:T(1024)S(1)} %pad_clamp_fusion), kind=kCustom, calls=%fused_computation.1.clone | custom fusion | bytes 426240 | tf_op jit(solution)/shard_map/jit(_take)/gather | solution.py:351
  5.6 0.0 copy-done.1
  5.6 0.8 gather_fusion
  6.4 0.0 copy-start.3
  6.4 0.1 broadcast_select_fusion
  6.5 0.8 reshape.107.refs_1_
  7.3 0.8 reshape.106.refs_0_
  8.0 39.1 %shard_map.94 = (bf16[32,2,1664]{2,1,0:T(2,128)(2,1)}, bf16[32,2,1664]{2,1,0:T(2,128)(2,1)}) custom-call(bf16[32,2,1664]{2,1,0:T(2,128)(2,1)} %reshape.106.refs_0_, bf16[32,2,1664]{2,1,0:T(2,128)(2,1)} %reshape.107.refs_1_), custom_call_target="tpu_custom_call" | custom-call | tf_op jit(solution)/shard_map/pallas_call | solution.py:106
  47.2 1.0 reshape.108
  48.2 0.9 convolution_convert_fusion.5.in_ref
  49.1 1.0 reshape.109
  50.1 0.0 copy-done.3
  50.1 0.9 fusion.3.grad_ref
  51.1 27.8 %shard_map.95 = (bf16[16,32,1664]{2,1,0:T(8,128)(2,1)}, bf16[16,32,1664]{2,1,0:T(8,128)(2,1)}) custom-call(bf16[32,1664]{1,0:T(8,128)(2,1)} %convolution_convert_fusion.5.in_ref, bf16[32,1664]{1,0:T(8,128)(2,1)} %fusion.3.grad_ref), custom_call_target="tpu_custom_call" | custom-call | tf_op jit(solution)/shard_map/pallas_call | solution.py:224
  78.9 0.0 copy-done
  78.9 0.0 copy-start.2
  78.9 0.0 copy-start.5
  78.9 2.2 %fusion.6 = f32[512,256]{1,0:T(8,128)S(1)} fusion(bf16[512,1664]{1,0:T(8,128)(2,1)} %bitcast.43, bf16[1,1664,256]{2,1,0:T(8,128)(2,1)S(1)} %copy-done), kind=kOutput, calls=%fused_computation.16 | convolution fusion | flops 436207616 | bytes 3080192 | tf_op jit(solution)/shard_map/dot_general | solution.py:375
  81.2 0.0 copy-done.2
  81.2 0.0 copy-done.5
  81.2 0.8 fusion.4
  82.0 0.0 copy-start.4
  82.0 1.6 %fusion.1 = bf16[1,256,1664]{2,1,0:T(8,128)(2,1)} fusion(bf16[512,1664]{1,0:T(8,128)(2,1)S(1)} %bitcast.41, f32[512,256]{1,0:T(8,128)S(1)} %fusion.6), kind=kOutput, calls=%fused_computation.6 | convolution fusion | flops 437813248 | bytes 3080192 | tf_op jit(solution)/shard_map/dot_general | solution.py:386
  83.6 0.0 copy-done.4
  83.6 1.6 %fusion = bf16[1,1664,256]{2,1,0:T(8,128)(2,1)} fusion(bf16[512,1664]{1,0:T(8,128)(2,1)S(1)} %bitcast.44, bf16[512,256]{1,0:T(8,128)(2,1)S(1)} %fusion.4), kind=kOutput, calls=%fused_computation.5 | convolution fusion | flops 436633600 | bytes 2818048 | tf_op jit(solution)/shard_map/dot_general | solution.py:389
  85.2 1.9 %convolution_convert_fusion = bf16[512,1664]{1,0:T(8,128)(2,1)} fusion(bf16[512,256]{1,0:T(8,128)(2,1)S(1)} %fusion.4, bf16[1,1664,256]{2,1,0:T(8,128)(2,1)S(1)} %copy-done), kind=kOutput, calls=%fused_computation.2 | convolution fusion | flops 437059584 | bytes 2818048 | tf_op jit(solution)/shard_map/dot_general | solution.py:382
  87.1 17.4 %shard_map.96 = bf16[32,1664]{1,0:T(8,128)(2,1)} custom-call(bf16[4,4,32,1664]{3,2,1,0:T(8,128)(2,1)} %bitcast.37), custom_call_target="tpu_custom_call" | custom-call | tf_op jit(solution)/shard_map/pallas_call | solution.py:322
  104.5 1.2 convolution_convert_fusion.4
  105.6 0.8 reshape.113.refs_0_
  106.4 24.9 %shard_map.97 = bf16[32,2,1664]{2,1,0:T(2,128)(2,1)} custom-call(bf16[32,2,1664]{2,1,0:T(2,128)(2,1)} %reshape.113.refs_0_), custom_call_target="tpu_custom_call" | custom-call | tf_op jit(solution)/shard_map/pallas_call | solution.py:106
  131.3 1.0 reshape.114
  132.3 1.0 fusion.2
  (3 shorter events, 0.0 us)
Async XLA Ops:
  0.6 78.3 %copy-start = (bf16[1,1664,256]{2,1,0:T(8,128)(2,1)S(1)}, bf16[1,1664,256]{2,1,0:T(8,128)(2,1)}, u32[]{:S(2)}) copy-start(bf16[1,1664,256]{2,1,0:T(8,128)(2,1)} %param.11) | copy-start | bytes 2555908
  0.6 5.0 %copy-start.1 = (bf16[1,1,128,1664]{3,2,1,0:T(8,128)(2,1)S(1)}, bf16[1,1,128,1664]{3,2,1,0:T(8,128)(2,1)}, u32[]{:S(2)}) copy-start(bf16[1,1,128,1664]{3,2,1,0:T(8,128)(2,1)} %param.9) | copy-start | bytes 1277956
  6.4 43.8 %copy-start.3 = (f32[1,1,32]{2,1,0:T(1,128)S(1)}, f32[1,1,32]{2,1,0:T(1,128)}, u32[]{:S(2)}) copy-start(f32[1,1,32]{2,1,0:T(1,128)} %param.13) | copy-start | bytes 388
  78.9 2.3 %copy-start.2 = (bf16[16,32,1664]{2,1,0:T(8,128)(2,1)S(1)}, bf16[16,32,1664]{2,1,0:T(8,128)(2,1)}, u32[]{:S(2)}) copy-start(bf16[16,32,1664]{2,1,0:T(8,128)(2,1)} %get-tuple-element.10) | copy-start | bytes 5111812
  78.9 2.3 %copy-start.5 = (bf16[1,256,1664]{2,1,0:T(8,128)(2,1)S(1)}, bf16[1,256,1664]{2,1,0:T(8,128)(2,1)}, u32[]{:S(2)}) copy-start(bf16[1,256,1664]{2,1,0:T(8,128)(2,1)} %param.12) | copy-start | bytes 2555908
  82.0 1.6 %copy-start.4 = (bf16[16,32,1664]{2,1,0:T(8,128)(2,1)S(1)}, bf16[16,32,1664]{2,1,0:T(8,128)(2,1)}, u32[]{:S(2)}) copy-start(bf16[16,32,1664]{2,1,0:T(8,128)(2,1)} %get-tuple-element.11) | copy-start | bytes 5111812

commit v2 on v0

v2 whole, which is shorter than its diff:
```python
import jax
import jax.numpy as jnp
from jax import lax
from jax.experimental import pallas as pl
from jax.experimental.pallas import tpu as pltpu
from jax.sharding import PartitionSpec as P

MESH = pl.DeviceIdType.MESH
SIDE = 4
HALF = 16
SPLIT = 896
BF16 = jnp.bfloat16
F32 = jnp.float32

gelu_scale = 0.7978845608028654
gelu_cubic = 0.044715


def gelu_parts(preact):
    inner_arg = gelu_scale * (preact + gelu_cubic * preact * preact * preact)
    tangent = jnp.tanh(inner_arg)
    gelu_value = 0.5 * preact * (1.0 + tangent)
    gelu_slope = 0.5 * (1.0 + tangent) + 0.5 * preact * (1.0 - tangent * tangent) * gelu_scale * (
        1.0 + 3.0 * gelu_cubic * preact * preact
    )
    return (gelu_value, gelu_slope)


def wrap(value):
    return lax.rem(value + 2 * SIDE, SIDE)


def place(half, first, second):
    return first * SIDE + second if half == 0 else second * SIDE + first


def one_hot(left, right):
    return (left == right).astype(BF16)


def layer_kernel(
    patches_hbm,
    grad_hbm,
    win_hbm,
    wout_hbm,
    gates,
    pick_col,
    pick_row,
    slot_col,
    slot_row,
    out_patches,
    out_win,
    out_wout,
    patches,
    grads,
    w_in,
    w_out,
    send,
    recv,
    mine,
    full,
    hidden,
    slope,
    grad_pre,
    parts,
    near,
    passing,
    summed,
    last,
    load_sem,
    own_sem,
    cross_send,
    cross_recv,
    spread_send,
    spread_recv,
    sum_send,
    sum_recv,
):
    experts = send.shape[1]
    width = patches.shape[1]
    me = lax.axis_index("expert")
    group = lax.axis_index("dp")
    spot_x, spot_y = lax.div(group, SIDE), lax.rem(group, SIDE)
    barrier = pltpu.get_barrier_semaphore()

    def offset_of(step):
        sign = 1 - 2 * lax.rem(step, 2)
        return experts // 2 + sign * lax.div(step + 1, 2)

    def greet(step, carry):
        peer = lax.rem(me + offset_of(step), experts)
        pl.semaphore_signal(barrier, inc=1, device_id={"expert": peer}, device_id_type=MESH)
        return carry

    lax.fori_loop(0, experts - 1, greet, 0)
    for shift in (1, -1, 2):
        for half in range(2):
            first, second = (spot_x, spot_y) if half == 0 else (spot_y, spot_x)
            pl.semaphore_signal(
                barrier,
                inc=1,
                device_id={"dp": place(half, wrap(first + shift), second)},
                device_id_type=MESH,
            )

    loads = [
        pltpu.make_async_copy(source, target, load_sem.at[i])
        for i, (source, target) in enumerate(
            ((patches_hbm, patches), (grad_hbm, grads), (win_hbm, w_in), (wout_hbm, w_out))
        )
    ]
    for load in loads:
        load.start()

    def cross(i, step, incoming):
        offset = offset_of(step)
        peer = lax.rem(me + (experts - offset if incoming else offset), experts)
        return pltpu.make_async_remote_copy(
            src_ref=send.at[i, peer],
            dst_ref=recv.at[i, peer if incoming else me],
            send_sem=cross_send.at[i, offset],
            recv_sem=cross_recv.at[i, offset],
            device_id={"expert": peer},
            device_id_type=MESH,
        )

    def own_block(i):
        return pltpu.make_async_copy(send.at[i, me], recv.at[i, me], own_sem.at[i])

    def cross_start(i):
        def launch(step, carry):
            cross(i, step, False).start()
            return carry

        lax.fori_loop(0, experts - 1, launch, 0)
        own_block(i).start()

    def cross_wait(i):
        def finish(step, carry):
            cross(i, step, True).wait_recv()
            return carry

        lax.fori_loop(0, experts - 1, finish, 0)
        own_block(i).wait()

    def cross_sent(i):
        def finish(step, carry):
            cross(i, step, False).wait_send()
            return carry

        lax.fori_loop(0, experts - 1, finish, 0)

    pick_hits = one_hot(
        pick_col[...], lax.broadcasted_iota(jnp.int32, (pick_col.shape[0], patches.shape[0]), 1)
    )
    for i, rows in ((0, patches), (1, grads)):
        loads[i].wait()
        chosen = jnp.dot(pick_hits, rows[...], preferred_element_type=F32).astype(BF16)
        send[i] = chosen.reshape(send.shape[1:])
    pl.semaphore_wait(barrier, experts - 1 + 6)
    cross_start(0)
    cross_start(1)

    slot_hits = one_hot(
        lax.broadcasted_iota(jnp.int32, (mine.shape[1], slot_row.shape[1]), 0), slot_row[...]
    )

    def compact(i):
        rows = recv[i].reshape(slot_row.shape[1], width)
        return jnp.dot(slot_hits, rows, preferred_element_type=F32)

    def piece(which, half, stage, move, incoming):
        way = (1, -1, 1, -1)[move]
        first, second = (spot_x, spot_y) if half == 0 else (spot_y, spot_x)
        rows = pl.ds(half * HALF, HALF)
        columns = (
            pl.ds(0, width),
            pl.ds(0, width),
            pl.ds(0, SPLIT),
            pl.ds(SPLIT, width - SPLIT),
        )[move]
        back = (0 if move < 2 else -way) - (way if incoming else 0)
        if stage == 0:
            block = place(half, wrap(first + back), second)
            peer = place(half, wrap(first + way), second)
        else:
            held = wrap(first + (0, -1, 1, 2)[stage - 1])
            block = place(half, held, wrap(second + back))
            peer = place(half, first, wrap(second + way))
        target = full.at[which, block, rows, columns]
        source = target
        if not incoming and move < 2 and stage < 2:
            source = mine.at[which, rows, columns]
        return pltpu.make_async_remote_copy(
            src_ref=source,
            dst_ref=target,
            send_sem=spread_send.at[which, half, stage, move],
            recv_sem=spread_recv.at[which, half, stage, move],
            device_id={"dp": peer},
            device_id_type=MESH,
        )

    def launch(which, half, stage, *moves):
        for move in moves:
            piece(which, half, stage, move, False).start()

    def arrive(which, half, stage, move):
        piece(which, half, stage, move, True).wait_recv()

    def relay(which, half, stage):
        arrive(which, half, stage, 0)
        launch(which, half, stage, 2)
        arrive(which, half, stage, 1)
        launch(which, half, stage, 3)

    def own_rows(which):
        return pltpu.make_async_copy(mine.at[which], full.at[which, group], own_sem.at[3 + which])

    halves = range(2)

    def spread_one(which):
        for stage in (0, 1):
            for half in halves:
                launch(which, half, stage, 0, 1)
        own_rows(which).start()

    def spread_two(which):
        for half in halves:
            arrive(which, half, 0, 0)
            launch(which, half, 0, 2)
            launch(which, half, 2, 0, 1)
            arrive(which, half, 0, 1)
            launch(which, half, 0, 3)
            launch(which, half, 3, 0, 1)

    def spread_three(which):
        for half in halves:
            relay(which, half, 1)
        for half in halves:
            arrive(which, half, 0, 2)
            arrive(which, half, 0, 3)
            launch(which, half, 4, 0, 1)

    def spread_four(which):
        for stage in (2, 3, 4):
            for half in halves:
                relay(which, half, stage)

    def spread_five(which):
        for stage in (1, 2, 3, 4):
            for half in halves:
                arrive(which, half, stage, 2)
                arrive(which, half, stage, 3)
        own_rows(which).wait()

    def spread_sent(which):
        for stage in range(5):
            for half in halves:
                for move in range(4):
                    piece(which, half, stage, move, False).wait_send()

    def stacked(which, chunk):
        rows = full[which, pl.ds(SIDE * chunk, SIDE)]
        return rows.reshape(SIDE * rows.shape[1], width)

    def forward(chunk):
        preact = jnp.dot(stacked(0, chunk), w_in[...], preferred_element_type=F32)
        gelu_value, gelu_slope = gelu_parts(preact)
        hidden[chunk] = gelu_value.astype(BF16)
        slope[chunk] = gelu_slope

    def backward(chunk):
        grad_hidden = lax.dot_general(
            stacked(1, chunk), w_out[...], (((1,), (1,)), ((), ())), preferred_element_type=F32
        )
        value = (grad_hidden * slope[chunk]).astype(BF16)
        grad_pre[chunk] = value
        partial = lax.dot_general(
            value, w_in[...], (((1,), (1,)), ((), ())), preferred_element_type=F32
        )
        parts[chunk] = partial.astype(BF16).reshape(parts.shape[1:])

    cross_wait(0)
    mine[0] = compact(0).astype(BF16)
    spread_one(0)
    spread_two(0)
    spread_three(0)
    spread_four(0)
    spread_five(0)
    loads[2].wait()
    forward(0)
    forward(1)
    cross_wait(1)
    mine[1] = (gates[...] * compact(1)).astype(BF16)
    spread_one(1)
    forward(2)
    spread_two(1)
    forward(3)
    spread_three(1)
    spread_four(1)
    spread_five(1)
    loads[3].wait()

    def unit(half, spot, begin=0, count=SIDE):
        rows = pl.ds(half * HALF, HALF)
        if half == 0:
            return parts.at[spot, pl.ds(begin, count), rows, :]
        return parts.at[pl.ds(begin, count), spot, rows, :]

    def gather_sum(half, move):
        first, second = (spot_x, spot_y) if half == 0 else (spot_y, spot_x)
        if move == 0:
            way, source, target = 1, unit(half, wrap(first + 1)), near.at[half, 0]
        elif move == 1:
            way, source, target = -1, unit(half, wrap(first - 1)), near.at[half, 1]
        elif move == 2:
            way, source, target = 1, unit(half, wrap(first + 2), 0, 2), passing.at[half, 0]
        elif move == 3:
            way, source, target = -1, unit(half, wrap(first + 2), 2, 2), passing.at[half, 1]
        elif move == 4:
            way, source, target = 1, passing.at[half, 0], near.at[half, 2, pl.ds(0, 2)]
        elif move == 5:
            way, source, target = -1, passing.at[half, 1], near.at[half, 2, pl.ds(2, 2)]
        else:
            way = (1, -1, 2)[move - 6]
            source, target = summed.at[half, wrap(second + way)], last.at[half, move - 6]
        if move < 6:
            peer = place(half, wrap(first + way), second)
        else:
            peer = place(half, first, wrap(second + way))
        return pltpu.make_async_remote_copy(
            src_ref=source,
            dst_ref=target,
            send_sem=sum_send.at[half, move],
            recv_sem=sum_recv.at[half, move],
            device_id={"dp": peer},
            device_id_type=MESH,
        )

    backward(wrap(spot_x + 2))
    gather_sum(0, 2).start()
    gather_sum(0, 3).start()
    backward(wrap(spot_x + 1))
    gather_sum(0, 0).start()
    backward(wrap(spot_x - 1))
    gather_sum(0, 1).start()
    backward(spot_x)
    for move in (2, 3, 0, 1):
        gather_sum(1, move).start()
    hidden_rows = hidden[...].reshape(hidden.shape[0] * hidden.shape[1], hidden.shape[2])
    grad_rows = grad_pre[...].reshape(hidden_rows.shape)

    def weight_out(begin, count):
        rows = full[1, :, :, begin : begin + count].reshape(hidden_rows.shape[0], count)
        out_wout[:, begin : begin + count] = lax.dot_general(
            hidden_rows, rows, (((0,), (0,)), ((), ())), preferred_element_type=F32
        ).astype(BF16)

    def weight_in(begin, count):
        rows = full[0, :, :, begin : begin + count].reshape(hidden_rows.shape[0], count)
        out_win[begin : begin + count, :] = lax.dot_general(
            rows, grad_rows, (((0,), (0,)), ((), ())), preferred_element_type=F32
        ).astype(BF16)

    for half in halves:
        gather_sum(half, 2).wait_recv()
        gather_sum(half, 4).start()
        gather_sum(half, 3).wait_recv()
        gather_sum(half, 5).start()
    weight_out(0, width)
    for half in halves:
        for move in (0, 1, 4, 5):
            gather_sum(half, move).wait_recv()
        index = spot_x if half == 0 else spot_y
        for spot in range(SIDE):
            rows = slice(half * HALF, half * HALF + HALF)
            own = parts[index, spot, rows, :] if half == 0 else parts[spot, index, rows, :]
            value = own.astype(F32)
            for source in range(3):
                value = value + near[half, source, spot].astype(F32)
            summed[half, spot] = value.astype(BF16)
        for move in (8, 6, 7):
            gather_sum(half, move).start()
    totals = []
    for half in halves:
        for move in (6, 7, 8):
            gather_sum(half, move).wait_recv()
        index = spot_y if half == 0 else spot_x
        value = summed[half, index].astype(F32)
        for source in range(3):
            value = value + last[half, source].astype(F32)
        totals.append(value.astype(BF16))
    total = jnp.concatenate(totals, axis=0)
    give_hits = one_hot(
        slot_col[...], lax.broadcasted_iota(jnp.int32, (slot_col.shape[0], total.shape[0]), 1)
    )
    returned = jnp.dot(give_hits, total, preferred_element_type=F32).astype(BF16)
    send[2] = returned.reshape(send.shape[1:])
    cross_start(2)
    weight_in(0, SPLIT)
    weight_in(SPLIT, width - SPLIT)
    spread_sent(0)
    spread_sent(1)
    for half in halves:
        for move in range(9):
            gather_sum(half, move).wait_send()
    cross_sent(0)
    cross_sent(1)
    cross_wait(2)
    owner_hits = one_hot(
        lax.broadcasted_iota(jnp.int32, (out_patches.shape[0], pick_row.shape[1]), 0),
        pick_row[...],
    )
    back = recv[2].reshape(pick_row.shape[1], width)
    out_patches[...] = jnp.dot(owner_hits, back, preferred_element_type=F32).astype(BF16)
    cross_sent(2)


def on_device(patches, grad_out, weight_in, weight_out, gates, counts, picks):
    tok_local = patches.shape[2]
    width = patches.shape[3]
    experts = picks.shape[2]
    per_owner = picks.shape[3]
    groups = counts.shape[0]
    owners = counts.shape[1]
    capacity = gates.shape[2]
    units = weight_in.shape[2]
    chosen = picks[0, 0].reshape(experts * per_owner)
    group_index = lax.axis_index("dp")
    my_counts = lax.dynamic_index_in_dim(counts[:, :, 0], group_index, 0, keepdims=False)
    my_begins = jnp.cumsum(my_counts) - my_counts
    rank_ids = jnp.arange(per_owner, dtype=jnp.int32)
    is_valid = rank_ids[None, :] < my_counts[:, None]
    slot_of = jnp.where(is_valid, my_begins[:, None] + rank_ids[None, :], -1)
    slot_of = slot_of.reshape(owners * per_owner)
    in_vmem = pl.BlockSpec(memory_space=pltpu.VMEM)
    in_place = pl.BlockSpec(memory_space=pl.ANY)
    rows = groups * capacity
    side_rows = rows // SIDE
    slab = (experts, per_owner, width)
    grad_patches, grad_in, grad_out_weight = pl.pallas_call(
        layer_kernel,
        out_shape=[
            jax.ShapeDtypeStruct((tok_local, width), BF16),
            jax.ShapeDtypeStruct((width, units), BF16),
            jax.ShapeDtypeStruct((units, width), BF16),
        ],
        in_specs=[in_place] * 4 + [in_vmem] * 5,
        out_specs=[in_vmem] * 3,
        scratch_shapes=[
            pltpu.VMEM((tok_local, width), BF16),
            pltpu.VMEM((tok_local, width), BF16),
            pltpu.VMEM((width, units), BF16),
            pltpu.VMEM((units, width), BF16),
            pltpu.VMEM((3,) + slab, BF16),
            pltpu.VMEM((3,) + slab, BF16),
            pltpu.VMEM((2, capacity, width), BF16),
            pltpu.VMEM((2, groups, capacity, width), BF16),
            pltpu.VMEM((SIDE, side_rows, units), BF16),
            pltpu.VMEM((SIDE, side_rows, units), F32),
            pltpu.VMEM((SIDE, side_rows, units), BF16),
            pltpu.VMEM((SIDE, SIDE, capacity, width), BF16),
            pltpu.VMEM((2, 3, SIDE, HALF, width), BF16),
            pltpu.VMEM((2, 2, 2, HALF, width), BF16),
            pltpu.VMEM((2, SIDE, HALF, width), BF16),
            pltpu.VMEM((2, 3, HALF, width), BF16),
            pltpu.SemaphoreType.DMA((4,)),
            pltpu.SemaphoreType.DMA((5,)),
            pltpu.SemaphoreType.DMA((3, experts)),
            pltpu.SemaphoreType.DMA((3, experts)),
            pltpu.SemaphoreType.DMA((2, 2, 5, 4)),
            pltpu.SemaphoreType.DMA((2, 2, 5, 4)),
            pltpu.SemaphoreType.DMA((2, 9)),
            pltpu.SemaphoreType.DMA((2, 9)),
        ],
        compiler_params=pltpu.CompilerParams(
            collective_id=1, has_side_effects=True, vmem_limit_bytes=56 * 1024 * 1024
        ),
    )(
        patches[0, 0],
        grad_out[0, 0],
        weight_in[0],
        weight_out[0],
        gates[0, 0][:, None],
        chosen[:, None],
        chosen[None, :],
        slot_of[:, None],
        slot_of[None, :],
    )
    return (grad_patches[None, None], grad_in[None], grad_out_weight[None])


def solution(mesh):
    return jax.shard_map(
        on_device,
        mesh=mesh,
        in_specs=(
            P("dp", "expert", None, None),
            P("dp", "expert", None, None),
            P("expert", None, "dp"),
            P("expert", "dp", None),
            P("expert", "dp", None),
            P(None, None, "expert"),
            P("dp", "expert", None, None),
        ),
        out_specs=(P("dp", "expert", None, None), P("expert", None, "dp"), P("expert", "dp", None)),
        check_vma=False,
    )
```

time: 312 us -> 106 us (0.34)
  waiting for transfers between devices: 212 us -> 0 us
  Pallas kernels: 0 us -> 95.7 us
  blocking collectives: 36.1 us -> 0 us
  starting transfers between devices: 19.7 us -> 0 us
  matrix products: 15.7 us -> 0 us
  between operations: 14 us -> 0.66 us
    pallas_call x0 -> x1, Pallas kernels: none -> 95.7 us  [on_device(): pl.pallas_call(layer_kernel, out_shape=[jax.ShapeDtypeStruct((tok_local,...]
    all_gather x2 -> x0, waiting for transfers between devices: 91.5 us -> none  [the longest x1 63.5 us: on_device(): piece_grad = lax.all_gather(scaled_rows, 'dp', axis=0, tiled=True)]
    reduce_scatter x1 -> x0, waiting for transfers between devices: 87.9 us -> none  [on_device(): lax.psum_scatter(lax.dot_general(stash_rows, local_in, (((1,), (1,)), (()...]
    all_to_all x1 -> x0, blocking collectives: 36.1 us -> none  [on_device(): lax.all_to_all(send_in, 'expert', split_axis=0, concat_axis=0, tiled=True)]
    all_to_all x2 -> x0, waiting for transfers between devices: 32.1 us -> none  [the longest x1 18.8 us: on_device(): lax.all_to_all(send_grad, 'expert', split_axis=0, concat_axis=0, tiled=True)]
    all_to_all x2 -> x0, starting transfers between devices: 19.5 us -> none  [the longest x1 14.7 us: on_device(): lax.all_to_all(returned, 'expert', split_axis=0, concat_axis=0, tiled=True)]
    dot_general x6 -> x0, matrix products: 15.7 us -> none  [the longest x1 4.13 us: on_device(): lax.dot_general(piece_in, grad_pre, (((0,), (0,)), ((), ())), preferred_e...]
    gather x5 -> x0, local copies, waits for them, and re-layouts: 7.87 us -> none  [the longest x1 2 us: on_device(): jnp.take(patches[0, 0], chosen, axis=0)]
  transfers between devices with their start and end apart: 5 -> 0, of which waited for: 5 -> 0; matrix products, arithmetic and copies ran while one was open for 4% -> 0% of each run, Pallas kernels for 0% -> 0%
where the time goes in v2:
time: 106 us
  Pallas kernels  95.7 us (90%)
  local copies, waits for them, and re-layouts  8.41 us (8%)
    pallas_call x1, Pallas kernels, on_device(): pl.pallas_call(layer_kernel, out_shape=[jax.ShapeDtypeStruct((tok_local,...  95.7 us
    unnamed x12, local copies, waits for them, and re-layouts  4.34 us

profile of v2, /device:TPU:1, one launch (start us, length us, event | category | flops | bytes accessed | tf_op | source)
XLA Modules:
  0.0 105.7 jit_solution(4837456470893514143)
XLA Ops:
  0.6 0.7 fusion
  1.3 0.1 copy.18
  1.4 0.1 reduce-window.8
  1.4 0.1 reduce
  1.6 0.7 fusion.2
  2.2 0.1 add_select_fusion
  2.3 0.0 copy-start.2
  2.3 0.7 select_n.31.slot_row
  3.0 0.0 copy-done.2
  3.0 0.1 copy.16
  3.1 0.6 broadcast_in_dim_reshape_squeeze.7.pick_row
  3.7 0.7 broadcast_in_dim_reshape_squeeze.8.pick_col
  4.3 0.0 copy-start.3
  4.3 0.7 select_n.32.slot_col
  5.0 0.0 copy-done.3
  5.0 0.7 copy.19.gates
  5.7 95.7 %shard_map.94 = (bf16[128,1664]{1,0:T(8,128)(2,1)}, bf16[1664,256]{1,0:T(8,128)(2,1)}, bf16[256,1664]{1,0:T(8,128)(2,1)}) custom-call(bf16[128,1664]{1,0:T(8,128)(2,1)} %bitcast.21, bf16[128,1664]{1,0:T(8,128)(2,1)} %bitcast.22, bf16[1664,256]{1,0:T(8,128)(2,1)} %bitcast.17, bf16[256,1664]{1,0:T(8,128)(2,1)} %bitcast.18, f32[32,1]{1,0:T(8,128)} %copy.19.gates, ...), custom_call_target="tpu_custom_call" | custom-call | tf_op jit(solution)/shard_map/pallas_call | solution.py:441
  101.5 0.0 copy-start.1
  101.5 1.9 %copy.25 = bf16[1,1,128,1664]{3,2,1,0:T(8,128)(2,1)} copy(bf16[1,1,128,1664]{3,2,1,0:T(8,128)(2,1)} %bitcast.23) | data formatting | bytes 851968
  103.4 0.0 copy-done.1
  103.4 0.0 copy-start
  103.4 0.9 copy.26
  104.3 0.6 copy-done
  104.8 0.9 copy.27
Async XLA Ops:
  2.3 0.7 copy-start.2
  4.3 0.7 copy-start.3
  101.5 1.9 %copy-start.1 = (bf16[1664,256]{1,0:T(8,128)(2,1)S(1)}, bf16[1664,256]{1,0:T(8,128)(2,1)}, u32[]{:S(2)}) copy-start(bf16[1664,256]{1,0:T(8,128)(2,1)} %get-tuple-element.7) | copy-start | bytes 2555908
  103.4 1.5 %copy-start = (bf16[256,1664]{1,0:T(8,128)(2,1)S(1)}, bf16[256,1664]{1,0:T(8,128)(2,1)}, u32[]{:S(2)}) copy-start(bf16[256,1664]{1,0:T(8,128)(2,1)} %get-tuple-element.8) | copy-start | bytes 2555908

commit v3 on v2

v3 whole, which is shorter than its diff:
```python
import jax
import jax.numpy as jnp
from jax import lax
from jax.experimental import pallas as pl
from jax.experimental.pallas import tpu as pltpu
from jax.sharding import PartitionSpec as P

MESH = pl.DeviceIdType.MESH
SIDE = 4
HALF = 16
CUT = 896
BF16 = jnp.bfloat16
F32 = jnp.float32

gelu_scale = 0.7978845608028654
gelu_cubic = 0.044715


def gelu_parts(preact):
    inner_arg = gelu_scale * (preact + gelu_cubic * preact * preact * preact)
    tangent = jnp.tanh(inner_arg)
    gelu_value = 0.5 * preact * (1.0 + tangent)
    gelu_slope = 0.5 * (1.0 + tangent) + 0.5 * preact * (1.0 - tangent * tangent) * gelu_scale * (
        1.0 + 3.0 * gelu_cubic * preact * preact
    )
    return (gelu_value, gelu_slope)


def wrap(value):
    return lax.rem(value + 2 * SIDE, SIDE)


def place(half, first, second):
    return first * SIDE + second if half == 0 else second * SIDE + first


def widths_of(width):
    return ((0, width), (0, CUT), (CUT, width - CUT))


def pick_table(picks, tokens):
    ranks, experts = picks.shape
    total = ranks * experts
    owner = lax.broadcasted_iota(jnp.int32, (experts, total), 0)
    entry = lax.broadcasted_iota(jnp.int32, (experts, total), 1)
    row = jnp.zeros((1, total), F32)
    for rank in range(ranks):
        spread_out = (entry == ranks * owner + rank).astype(BF16)
        values = picks[rank : rank + 1, :].astype(F32).astype(BF16)
        row = row + jnp.dot(values, spread_out, preferred_element_type=F32)
    token = lax.broadcasted_iota(jnp.int32, (tokens, total), 0)
    return (token == row.astype(jnp.int32)).astype(BF16)


def slot_table(counts, capacity, ranks):
    owners = counts.shape[1]
    total = ranks * owners
    owner = lax.broadcasted_iota(jnp.int32, (owners, total), 0)
    entry = lax.broadcasted_iota(jnp.int32, (owners, total), 1)
    before = (ranks * owner + ranks <= entry).astype(BF16)
    here = ((ranks * owner <= entry) & (entry < ranks * owner + ranks)).astype(BF16)
    taken = counts.astype(F32).astype(BF16)
    begin = jnp.dot(taken, before, preferred_element_type=F32)
    count = jnp.dot(taken, here, preferred_element_type=F32)
    rank = lax.rem(lax.broadcasted_iota(jnp.int32, (1, total), 1), ranks).astype(F32)
    slot = jnp.where(rank < count, begin + rank, -1.0).astype(jnp.int32)
    row = lax.broadcasted_iota(jnp.int32, (capacity, total), 0)
    return (row == slot).astype(BF16)


def layer_kernel(*refs):
    (patches_hbm, grad_hbm, win_hbm, wout_hbm, gates, counts, picks) = refs[:7]
    back = refs[7:9]
    out_win, out_wout = refs[9:11]
    (patches, grads, w_in, w_out, hold_win, hold_wout) = refs[11:17]
    send = refs[17:22]
    recv = refs[22:25] + back
    mine = refs[25:28]
    full = refs[28:31]
    (hidden, slope, early, grad_pre) = refs[31:35]
    parts = refs[35:37]
    near = refs[37:39]
    passing = refs[39:41]
    summed = refs[41:43]
    last = refs[43:45]
    (load_sem, own_sem, cross_send, cross_recv) = refs[45:49]
    (spread_send, spread_recv, sum_send, sum_recv) = refs[49:]
    experts, ranks = send[0].shape[:2]
    capacity = mine[0].shape[0]
    width = patches.shape[1]
    spans = widths_of(width)
    me = lax.axis_index("expert")
    group = lax.axis_index("dp")
    spot_x, spot_y = lax.div(group, SIDE), lax.rem(group, SIDE)
    barrier = pltpu.get_barrier_semaphore()

    def offset_of(step):
        sign = 1 - 2 * lax.rem(step, 2)
        return experts // 2 + sign * lax.div(step + 1, 2)

    def greet(step, carry):
        peer = lax.rem(me + offset_of(step), experts)
        pl.semaphore_signal(barrier, inc=1, device_id={"expert": peer}, device_id_type=MESH)
        return carry

    lax.fori_loop(0, experts - 1, greet, 0)
    for shift in (1, -1, 2):
        for half in range(2):
            first, second = (spot_x, spot_y) if half == 0 else (spot_y, spot_x)
            pl.semaphore_signal(
                barrier,
                inc=1,
                device_id={"dp": place(half, wrap(first + shift), second)},
                device_id_type=MESH,
            )

    loads = [
        pltpu.make_async_copy(source, target, load_sem.at[i])
        for i, (source, target) in enumerate(
            ((patches_hbm, patches), (grad_hbm, grads), (win_hbm, w_in), (wout_hbm, w_out))
        )
    ]
    for load in loads:
        load.start()

    def cross(i, step, incoming):
        offset = offset_of(step)
        peer = lax.rem(me + (experts - offset if incoming else offset), experts)
        return pltpu.make_async_remote_copy(
            src_ref=send[i].at[peer],
            dst_ref=recv[i].at[peer if incoming else me],
            send_sem=cross_send.at[i, offset],
            recv_sem=cross_recv.at[i, offset],
            device_id={"expert": peer},
            device_id_type=MESH,
        )

    def own_block(i):
        return pltpu.make_async_copy(send[i].at[me], recv[i].at[me], own_sem.at[i])

    def cross_start(i):
        def launch(step, carry):
            cross(i, step, False).start()
            return carry

        lax.fori_loop(0, experts - 1, launch, 0)
        own_block(i).start()

    def cross_wait(i):
        def finish(step, carry):
            cross(i, step, True).wait_recv()
            return carry

        lax.fori_loop(0, experts - 1, finish, 0)
        own_block(i).wait()

    def cross_sent(i):
        def finish(step, carry):
            cross(i, step, False).wait_send()
            return carry

        lax.fori_loop(0, experts - 1, finish, 0)

    pick_hits = pick_table(picks, patches.shape[0])
    slot_hits = slot_table(counts[group], capacity, ranks)
    diagonal = lax.broadcasted_iota(jnp.int32, (capacity, capacity), 0) == (
        lax.broadcasted_iota(jnp.int32, (capacity, capacity), 1)
    )
    gate_col = jnp.sum(jnp.where(diagonal, gates[...], 0.0), axis=1, keepdims=True)

    def turned(left, right):
        return lax.dot_general(left, right, (((0,), (0,)), ((), ())), preferred_element_type=F32)

    loads[0].wait()
    send[0][...] = turned(pick_hits, patches[...]).astype(BF16).reshape(send[0].shape)
    loads[1].wait()
    chosen = turned(pick_hits, grads[...]).astype(BF16)
    for i in (1, 2):
        begin, count = spans[i]
        send[i][...] = chosen[:, begin : begin + count].reshape(send[i].shape)
    pl.semaphore_wait(barrier, experts - 1 + 6)
    for i in range(3):
        cross_start(i)

    def compact(i):
        rows = recv[i][...].reshape(ranks * experts, spans[i][1])
        return jnp.dot(slot_hits, rows, preferred_element_type=F32)

    def piece(which, half, stage, move, incoming):
        way = (1, -1, 1, -1)[move]
        first, second = (spot_x, spot_y) if half == 0 else (spot_y, spot_x)
        rows = pl.ds(half * HALF, HALF)
        wide = spans[which][1]
        split = (wide // 256 + 1) * 128 if wide % 256 else wide // 2
        columns = (pl.ds(0, wide), pl.ds(0, wide), pl.ds(0, split), pl.ds(split, wide - split))[
            move
        ]
        back_by = (0 if move < 2 else -way) - (way if incoming else 0)
        if stage == 0:
            block = place(half, wrap(first + back_by), second)
            peer = place(half, wrap(first + way), second)
        else:
            held = wrap(first + (0, -1, 1, 2)[stage - 1])
            block = place(half, held, wrap(second + back_by))
            peer = place(half, first, wrap(second + way))
        target = full[which].at[block, rows, columns]
        source = target
        if not incoming and move < 2 and stage < 2:
            source = mine[which].at[rows, columns]
        return pltpu.make_async_remote_copy(
            src_ref=source,
            dst_ref=target,
            send_sem=spread_send.at[which, half, stage, move],
            recv_sem=spread_recv.at[which, half, stage, move],
            device_id={"dp": peer},
            device_id_type=MESH,
        )

    def launch(which, half, stage, *moves):
        for move in moves:
            piece(which, half, stage, move, False).start()

    def arrive(which, half, stage, move):
        piece(which, half, stage, move, True).wait_recv()

    def relay(which, half, stage):
        arrive(which, half, stage, 0)
        launch(which, half, stage, 2)
        arrive(which, half, stage, 1)
        launch(which, half, stage, 3)

    def own_rows(which):
        return pltpu.make_async_copy(mine[which], full[which].at[group], own_sem.at[5 + which])

    halves = range(2)

    def spread_one(which):
        for stage in (0, 1):
            for half in halves:
                launch(which, half, stage, 0, 1)
        own_rows(which).start()

    def spread_two(which):
        for half in halves:
            arrive(which, half, 0, 0)
            launch(which, half, 0, 2)
            launch(which, half, 2, 0, 1)
            arrive(which, half, 0, 1)
            launch(which, half, 0, 3)
            launch(which, half, 3, 0, 1)

    def spread_three(which):
        for half in halves:
            relay(which, half, 1)
        for half in halves:
            arrive(which, half, 0, 2)
            arrive(which, half, 0, 3)
            launch(which, half, 4, 0, 1)

    def spread_four(which):
        for stage in (2, 3, 4):
            for half in halves:
                relay(which, half, stage)

    def spread_five(which):
        for stage in (1, 2, 3, 4):
            for half in halves:
                arrive(which, half, stage, 2)
                arrive(which, half, stage, 3)
        own_rows(which).wait()

    def spread_sent(which):
        for stage in range(5):
            for half in halves:
                for move in range(4):
                    piece(which, half, stage, move, False).wait_send()

    def stacked(which, chunk):
        rows = full[which][pl.ds(SIDE * chunk, SIDE)]
        return rows.reshape(SIDE * capacity, spans[which][1])

    def forward(chunk):
        preact = jnp.dot(stacked(0, chunk), w_in[...], preferred_element_type=F32)
        gelu_value, gelu_slope = gelu_parts(preact)
        hidden[chunk] = gelu_value.astype(BF16)
        slope[chunk] = gelu_slope

    def pull(which, chunk):
        begin, count = spans[which]
        return lax.dot_general(
            stacked(which, chunk),
            w_out[:, begin : begin + count],
            (((1,), (1,)), ((), ())),
            preferred_element_type=F32,
        )

    def backward(chunk):
        grad_hidden = early[chunk] + pull(2, chunk)
        grad_pre[chunk] = (grad_hidden * slope[chunk]).astype(BF16)

    def project(part, chunk):
        begin, count = spans[1 + part]
        partial = lax.dot_general(
            grad_pre[chunk],
            w_in[begin : begin + count, :],
            (((1,), (1,)), ((), ())),
            preferred_element_type=F32,
        )
        parts[part][chunk] = partial.astype(BF16).reshape(parts[part].shape[1:])

    cross_wait(0)
    mine[0][...] = compact(0).astype(BF16)
    spread_one(0)
    spread_two(0)
    spread_three(0)
    spread_four(0)
    spread_five(0)
    cross_wait(1)
    mine[1][...] = (gate_col * compact(1)).astype(BF16)
    spread_one(1)
    loads[2].wait()
    forward(0)
    spread_two(1)
    forward(1)
    spread_three(1)
    spread_four(1)
    spread_five(1)
    cross_wait(2)
    mine[2][...] = (gate_col * compact(2)).astype(BF16)
    spread_one(2)
    forward(2)
    spread_two(2)
    forward(3)
    spread_three(2)
    loads[3].wait()
    for chunk in range(SIDE):
        early[chunk] = pull(1, chunk)
    spread_four(2)
    spread_five(2)

    def unit(part, half, spot, begin=0, count=SIDE):
        rows = pl.ds(half * HALF, HALF)
        if half == 0:
            return parts[part].at[spot, pl.ds(begin, count), rows, :]
        return parts[part].at[pl.ds(begin, count), spot, rows, :]

    def tally(part, half, move):
        first, second = (spot_x, spot_y) if half == 0 else (spot_y, spot_x)
        close, through = near[part], passing[part]
        if move == 0:
            way, source, target = 1, unit(part, half, wrap(first + 1)), close.at[half, 0]
        elif move == 1:
            way, source, target = -1, unit(part, half, wrap(first - 1)), close.at[half, 1]
        elif move == 2:
            way, source, target = 1, unit(part, half, wrap(first + 2), 0, 2), through.at[half, 0]
        elif move == 3:
            way, source, target = -1, unit(part, half, wrap(first + 2), 2, 2), through.at[half, 1]
        elif move == 4:
            way, source, target = 1, through.at[half, 0], close.at[half, 2, pl.ds(0, 2)]
        elif move == 5:
            way, source, target = -1, through.at[half, 1], close.at[half, 2, pl.ds(2, 2)]
        else:
            way = (1, -1, 2)[move - 6]
            source = summed[part].at[half, wrap(second + way)]
            target = last[part].at[half, move - 6]
        if move < 6:
            peer = place(half, wrap(first + way), second)
        else:
            peer = place(half, first, wrap(second + way))
        return pltpu.make_async_remote_copy(
            src_ref=source,
            dst_ref=target,
            send_sem=sum_send.at[part, half, move],
            recv_sem=sum_recv.at[part, half, move],
            device_id={"dp": peer},
            device_id_type=MESH,
        )

    def tally_relay(part):
        for half in halves:
            tally(part, half, 2).wait_recv()
            tally(part, half, 4).start()
            tally(part, half, 3).wait_recv()
            tally(part, half, 5).start()

    def tally_near(part):
        for half in halves:
            for move in (0, 1, 4, 5):
                tally(part, half, move).wait_recv()
            index = spot_x if half == 0 else spot_y
            rows = slice(half * HALF, half * HALF + HALF)
            for spot in range(SIDE):
                if half == 0:
                    own = parts[part][index, spot, rows, :]
                else:
                    own = parts[part][spot, index, rows, :]
                value = own.astype(F32)
                for source in range(3):
                    value = value + near[part][half, source, spot].astype(F32)
                summed[part][half, spot] = value.astype(BF16)
            for move in (8, 6, 7):
                tally(part, half, move).start()

    def give_back(part):
        totals = []
        for half in halves:
            for move in (6, 7, 8):
                tally(part, half, move).wait_recv()
            index = spot_y if half == 0 else spot_x
            value = summed[part][half, index].astype(F32)
            for source in range(3):
                value = value + last[part][half, source].astype(F32)
            totals.append(value.astype(BF16))
        total = jnp.concatenate(totals, axis=0)
        send[3 + part][...] = turned(slot_hits, total).astype(BF16).reshape(send[3 + part].shape)
        cross_start(3 + part)

    backward(wrap(spot_x + 2))
    project(0, wrap(spot_x + 2))
    tally(0, 0, 2).start()
    tally(0, 0, 3).start()
    backward(wrap(spot_x + 1))
    project(0, wrap(spot_x + 1))
    tally(0, 0, 0).start()
    backward(wrap(spot_x - 1))
    project(0, wrap(spot_x - 1))
    tally(0, 0, 1).start()
    backward(spot_x)
    project(0, spot_x)
    for move in (2, 3, 0, 1):
        tally(0, 1, move).start()
    for chunk in range(SIDE):
        project(1, chunk)
    tally_relay(0)
    for move in (2, 3, 0, 1):
        for half in halves:
            tally(1, half, move).start()
    hidden_rows = hidden[...].reshape(SIDE * hidden.shape[1], hidden.shape[2])
    grad_rows = grad_pre[...].reshape(hidden_rows.shape)

    def weight_out(which):
        begin, count = spans[which]
        rows = full[which][...].reshape(hidden_rows.shape[0], count)
        hold_wout[:, begin : begin + count] = turned(hidden_rows, rows).astype(BF16)

    def weight_in(begin, count):
        rows = full[0][:, :, begin : begin + count].reshape(hidden_rows.shape[0], count)
        hold_win[begin : begin + count, :] = turned(rows, grad_rows).astype(BF16)

    weight_out(1)
    tally_near(0)
    tally_relay(1)
    give_back(0)
    tally_near(1)
    weight_out(2)
    give_back(1)
    store_wout = pltpu.make_async_copy(hold_wout, out_wout, load_sem.at[4])
    store_wout.start()
    weight_in(*spans[1])
    weight_in(*spans[2])
    store_win = pltpu.make_async_copy(hold_win, out_win, load_sem.at[5])
    store_win.start()
    for which in range(3):
        spread_sent(which)
    for part in range(2):
        for half in halves:
            for move in range(9):
                tally(part, half, move).wait_send()
    for i in range(3):
        cross_sent(i)
    cross_wait(3)
    cross_wait(4)
    cross_sent(3)
    cross_sent(4)
    store_wout.wait()
    store_win.wait()


def tail_kernel(
    picks, back_a, back_b, win_hbm, wout_hbm, out_patches, out_win, out_wout, win, wout, sem_in, sem_out
):
    width = out_patches.shape[1]
    loads, stores = [], []
    for i, (source, held, target) in enumerate(((win_hbm, win, out_win), (wout_hbm, wout, out_wout))):
        step = source.shape[0] // 2
        for half in range(2):
            rows = pl.ds(half * step, step)
            at = 2 * i + half
            loads.append(pltpu.make_async_copy(source.at[rows], held.at[rows], sem_in.at[at]))
            stores.append(pltpu.make_async_copy(held.at[rows], target.at[rows], sem_out.at[at]))
    for load in loads:
        load.start()
    owner_hits = pick_table(picks, out_patches.shape[0])
    for (begin, count), back in zip(widths_of(width)[1:], (back_a, back_b)):
        rows = back[...].reshape(back.shape[0] * back.shape[1], count)
        out_patches[:, begin : begin + count] = jnp.dot(
            owner_hits, rows, preferred_element_type=F32
        ).astype(BF16)
    for load, store in zip(loads, stores):
        load.wait()
        store.start()
    for store in stores:
        store.wait()


def on_device(patches, grad_out, weight_in, weight_out, gates, counts, picks):
    tokens = patches.shape[2]
    width = patches.shape[3]
    experts = picks.shape[2]
    ranks = picks.shape[3]
    groups = counts.shape[0]
    capacity = gates.shape[2]
    units = weight_in.shape[2]
    side_rows = groups * capacity // SIDE
    parts = [count for _, count in widths_of(width)]
    in_vmem = pl.BlockSpec(memory_space=pltpu.VMEM)
    in_place = pl.BlockSpec(memory_space=pl.ANY)
    shape_in = jax.ShapeDtypeStruct((width, units), BF16)
    shape_out = jax.ShapeDtypeStruct((units, width), BF16)
    local_picks = jnp.transpose(picks[0, 0])
    slabs = [pltpu.VMEM((experts, ranks, count), BF16) for count in parts + parts[1:]]
    back_a, back_b, grad_in, grad_out_weight = pl.pallas_call(
        layer_kernel,
        out_shape=[jax.ShapeDtypeStruct((experts, ranks, count), BF16) for count in parts[1:]]
        + [shape_in, shape_out],
        in_specs=[in_place] * 4 + [in_vmem] * 3,
        out_specs=[in_vmem] * 2 + [in_place] * 2,
        scratch_shapes=[
            pltpu.VMEM((tokens, width), BF16),
            pltpu.VMEM((tokens, width), BF16),
            pltpu.VMEM((width, units), BF16),
            pltpu.VMEM((units, width), BF16),
            pltpu.VMEM((width, units), BF16),
            pltpu.VMEM((units, width), BF16),
        ]
        + slabs
        + slabs[:3]
        + [pltpu.VMEM((capacity, count), BF16) for count in parts]
        + [pltpu.VMEM((groups, capacity, count), BF16) for count in parts]
        + [
            pltpu.VMEM((SIDE, side_rows, units), BF16),
            pltpu.VMEM((SIDE, side_rows, units), F32),
            pltpu.VMEM((SIDE, side_rows, units), F32),
            pltpu.VMEM((SIDE, side_rows, units), BF16),
        ]
        + [pltpu.VMEM((SIDE, SIDE, capacity, count), BF16) for count in parts[1:]]
        + [pltpu.VMEM((2, 3, SIDE, HALF, count), BF16) for count in parts[1:]]
        + [pltpu.VMEM((2, 2, 2, HALF, count), BF16) for count in parts[1:]]
        + [pltpu.VMEM((2, SIDE, HALF, count), BF16) for count in parts[1:]]
        + [pltpu.VMEM((2, 3, HALF, count), BF16) for count in parts[1:]]
        + [
            pltpu.SemaphoreType.DMA((6,)),
            pltpu.SemaphoreType.DMA((8,)),
            pltpu.SemaphoreType.DMA((5, experts)),
            pltpu.SemaphoreType.DMA((5, experts)),
            pltpu.SemaphoreType.DMA((3, 2, 5, 4)),
            pltpu.SemaphoreType.DMA((3, 2, 5, 4)),
            pltpu.SemaphoreType.DMA((2, 2, 9)),
            pltpu.SemaphoreType.DMA((2, 2, 9)),
        ],
        compiler_params=pltpu.CompilerParams(
            collective_id=1, has_side_effects=True, vmem_limit_bytes=56 * 1024 * 1024
        ),
    )(
        patches[0, 0],
        grad_out[0, 0],
        weight_in[0],
        weight_out[0],
        gates[0],
        jnp.transpose(counts, (0, 2, 1)),
        local_picks,
    )
    grad_patches, grad_in, grad_out_weight = pl.pallas_call(
        tail_kernel,
        out_shape=[jax.ShapeDtypeStruct((tokens, width), BF16), shape_in, shape_out],
        in_specs=[in_vmem] * 3 + [in_place] * 2,
        out_specs=[in_vmem] + [in_place] * 2,
        scratch_shapes=[
            pltpu.VMEM((width, units), BF16),
            pltpu.VMEM((units, width), BF16),
            pltpu.SemaphoreType.DMA((4,)),
            pltpu.SemaphoreType.DMA((4,)),
        ],
        compiler_params=pltpu.CompilerParams(vmem_limit_bytes=56 * 1024 * 1024),
    )(local_picks, back_a, back_b, grad_in, grad_out_weight)
    return (grad_patches[None, None], grad_in[None], grad_out_weight[None])


def solution(mesh):
    return jax.shard_map(
        on_device,
        mesh=mesh,
        in_specs=(
            P("dp", "expert", None, None),
            P("dp", "expert", None, None),
            P("expert", None, "dp"),
            P("expert", "dp", None),
            P("expert", "dp", None),
            P(None, None, "expert"),
            P("dp", "expert", None, None),
        ),
        out_specs=(P("dp", "expert", None, None), P("expert", None, "dp"), P("expert", "dp", None)),
        check_vma=False,
    )
```

time: 106 us -> 115 us (1.085)
  Pallas kernels: 95.7 us -> 114 us
  local copies, waits for them, and re-layouts: 8.41 us -> 0 us
    pallas_call x1 -> x2, Pallas kernels: 95.7 us -> 114 us  [the longest x1 110 us: on_device(): pl.pallas_call(layer_kernel, out_shape=[jax.ShapeDtypeStruct((experts, ra...]
    unnamed x12 -> x0, local copies, waits for them, and re-layouts: 4.34 us -> none
    another operation x5 -> x0, local copies, waits for them, and re-layouts: 2.71 us -> none
    select_n x2 -> x0, local copies, waits for them, and re-layouts: 1.36 us -> none  [on_device(): slot_of = jnp.where(is_valid, my_begins[:, None] + rank_ids[None, :], -1)]
where the time goes in v3:
time: 115 us
  Pallas kernels  114 us (99%)
    pallas_call x1, Pallas kernels, on_device(): pl.pallas_call(layer_kernel, out_shape=[jax.ShapeDtypeStruct((experts, ra...  110 us
    pallas_call x1, Pallas kernels, on_device(): pl.pallas_call(tail_kernel, out_shape=[jax.ShapeDtypeStruct((tokens, widt...  3.98 us

profile of v3, /device:TPU:1, one launch (start us, length us, event | category | flops | bytes accessed | tf_op | source)
XLA Modules:
  0.0 115.1 jit_solution(4981268674722694658)
XLA Ops:
  0.6 110.5 %shard_map.94 = (bf16[32,2,896]{2,1,0:T(2,128)(2,1)}, bf16[32,2,768]{2,1,0:T(2,128)(2,1)}, bf16[1664,256]{1,0:T(8,128)(2,1)}, bf16[256,1664]{1,0:T(8,128)(2,1)}) custom-call(bf16[128,1664]{1,0:T(8,128)(2,1)} %bitcast.14, bf16[128,1664]{1,0:T(8,128)(2,1)} %bitcast.15, bf16[1664,256]{1,0:T(8,128)(2,1)} %bitcast.12, bf16[256,1664]{1,0:T(8,128)(2,1)} %bitcast.13, ...), custom_call_target="tpu_custom_call" | custom-call | tf_op jit(solution)/shard_map/pallas_call | solution.py:522
  111.1 4.0 %shard_map.95 = (bf16[128,1664]{1,0:T(8,128)(2,1)}, bf16[1664,256]{1,0:T(8,128)(2,1)}, bf16[256,1664]{1,0:T(8,128)(2,1)}) custom-call(s32[2,32]{1,0:T(2,128)} %bitcast.18, bf16[32,2,896]{2,1,0:T(2,128)(2,1)} %get-tuple-element.10.back_a, bf16[32,2,768]{2,1,0:T(2,128)(2,1)} %get-tuple-element.11.back_b, bf16[1664,256]{1,0:T(8,128)(2,1)} %get-tuple-element.12.win_hbm, ...), custom_call_target="tpu_custom_call" | custom-call | tf_op jit(solution)/shard_map/pallas_call | solution.py:573

commit v4 on v3

--- a/solution.py
+++ b/solution.py
@@ -35,7 +35,7 @@
 
 
 def widths_of(width):
-    return ((0, width), (0, CUT), (CUT, width - CUT))
+    return ((0, width), (0, width))
 
 
 def pick_table(picks, tokens):
@@ -70,21 +70,16 @@
 
 def layer_kernel(*refs):
     (patches_hbm, grad_hbm, win_hbm, wout_hbm, gates, counts, picks) = refs[:7]
-    back = refs[7:9]
-    out_win, out_wout = refs[9:11]
-    (patches, grads, w_in, w_out, hold_win, hold_wout) = refs[11:17]
-    send = refs[17:22]
-    recv = refs[22:25] + back
-    mine = refs[25:28]
-    full = refs[28:31]
-    (hidden, slope, early, grad_pre) = refs[31:35]
-    parts = refs[35:37]
-    near = refs[37:39]
-    passing = refs[39:41]
-    summed = refs[41:43]
-    last = refs[43:45]
-    (load_sem, own_sem, cross_send, cross_recv) = refs[45:49]
-    (spread_send, spread_recv, sum_send, sum_recv) = refs[49:]
+    back = refs[7:8]
+    out_win, out_wout = refs[8:10]
+    (patches, grads, w_in, w_out, hold_win, hold_wout) = refs[10:16]
+    send = refs[16:19]
+    recv = refs[19:21] + back
+    mine = refs[21:23]
+    full = refs[23:25]
+    (hidden, slope, grad_pre, parts, near, passing, summed, last) = refs[25:33]
+    (load_sem, own_sem, cross_send, cross_recv) = refs[33:37]
+    (spread_send, spread_recv, sum_send, sum_recv) = refs[37:]
     experts, ranks = send[0].shape[:2]
     capacity = mine[0].shape[0]
     width = patches.shape[1]
@@ -138,13 +133,14 @@
     def own_block(i):
         return pltpu.make_async_copy(send[i].at[me], recv[i].at[me], own_sem.at[i])
 
-    def cross_start(i):
+    def cross_start(i, begin=0, end=experts - 1):
         def launch(step, carry):
             cross(i, step, False).start()
             return carry
 
-        lax.fori_loop(0, experts - 1, launch, 0)
-        own_block(i).start()
+        lax.fori_loop(begin, end, launch, 0)
+        if begin == 0:
+            own_block(i).start()
 
     def cross_wait(i):
         def finish(step, carry):
@@ -174,13 +170,10 @@
     loads[0].wait()
     send[0][...] = turned(pick_hits, patches[...]).astype(BF16).reshape(send[0].shape)
     loads[1].wait()
-    chosen = turned(pick_hits, grads[...]).astype(BF16)
-    for i in (1, 2):
-        begin, count = spans[i]
-        send[i][...] = chosen[:, begin : begin + count].reshape(send[i].shape)
+    send[1][...] = turned(pick_hits, grads[...]).astype(BF16).reshape(send[1].shape)
     pl.semaphore_wait(barrier, experts - 1 + 6)
-    for i in range(3):
-        cross_start(i)
+    cross_start(0)
+    cross_start(1)
 
     def compact(i):
         rows = recv[i][...].reshape(ranks * experts, spans[i][1])
@@ -230,7 +223,7 @@
         launch(which, half, stage, 3)
 
     def own_rows(which):
-        return pltpu.make_async_copy(mine[which], full[which].at[group], own_sem.at[5 + which])
+        return pltpu.make_async_copy(mine[which], full[which].at[group], own_sem.at[3 + which])
 
     halves = range(2)
 
@@ -285,84 +278,63 @@
         hidden[chunk] = gelu_value.astype(BF16)
         slope[chunk] = gelu_slope
 
-    def pull(which, chunk):
-        begin, count = spans[which]
-        return lax.dot_general(
-            stacked(which, chunk),
-            w_out[:, begin : begin + count],
-            (((1,), (1,)), ((), ())),
-            preferred_element_type=F32,
+    def backward(chunk):
+        grad_hidden = lax.dot_general(
+            stacked(1, chunk), w_out[...], (((1,), (1,)), ((), ())), preferred_element_type=F32
         )
-
-    def backward(chunk):
-        grad_hidden = early[chunk] + pull(2, chunk)
-        grad_pre[chunk] = (grad_hidden * slope[chunk]).astype(BF16)
-
-    def project(part, chunk):
-        begin, count = spans[1 + part]
+        value = (grad_hidden * slope[chunk]).astype(BF16)
+        grad_pre[chunk] = value
         partial = lax.dot_general(
-            grad_pre[chunk],
-            w_in[begin : begin + count, :],
-            (((1,), (1,)), ((), ())),
-            preferred_element_type=F32,
+            value, w_in[...], (((1,), (1,)), ((), ())), preferred_element_type=F32
         )
-        parts[part][chunk] = partial.astype(BF16).reshape(parts[part].shape[1:])
+        parts[chunk] = partial.astype(BF16).reshape(parts.shape[1:])
 
     cross_wait(0)
     mine[0][...] = compact(0).astype(BF16)
     spread_one(0)
     spread_two(0)
     spread_three(0)
-    spread_four(0)
-    spread_five(0)
     cross_wait(1)
     mine[1][...] = (gate_col * compact(1)).astype(BF16)
     spread_one(1)
+    spread_four(0)
+    spread_five(0)
+    spread_two(1)
     loads[2].wait()
     forward(0)
-    spread_two(1)
+    spread_three(1)
     forward(1)
-    spread_three(1)
     spread_four(1)
+    forward(2)
+    forward(3)
     spread_five(1)
-    cross_wait(2)
-    mine[2][...] = (gate_col * compact(2)).astype(BF16)
-    spread_one(2)
-    forward(2)
-    spread_two(2)
-    forward(3)
-    spread_three(2)
     loads[3].wait()
-    for chunk in range(SIDE):
-        early[chunk] = pull(1, chunk)
-    spread_four(2)
-    spread_five(2)
-
-    def unit(part, half, spot, begin=0, count=SIDE):
+
+    def unit(half, spot, begin=0, count=SIDE):
         rows = pl.ds(half * HALF, HALF)
         if half == 0:
-            return parts[part].at[spot, pl.ds(begin, count), rows, :]
-        return parts[part].at[pl.ds(begin, count), spot, rows, :]
-
-    def tally(part, half, move):
+            return parts.at[spot, pl.ds(begin, count), rows, :]
+        return parts.at[pl.ds(begin, count), spot, rows, :]
+
+    def tally(half, move):
         first, second = (spot_x, spot_y) if half == 0 else (spot_y, spot_x)
-        close, through = near[part], passing[part]
+        close, through = near, passing
         if move == 0:
-            way, source, target = 1, unit(part, half, wrap(first + 1)), close.at[half, 0]
+            way, source, target = 1, unit(half, wrap(first + 1)), close.at[half, 0]
         elif move == 1:
-            way, source, target = -1, unit(part, half, wrap(first - 1)), close.at[half, 1]
+            way, source, target = -1, unit(half, wrap(first - 1)), close.at[half, 1]
         elif move == 2:
-            way, source, target = 1, unit(part, half, wrap(first + 2), 0, 2), through.at[half, 0]
+            way, source, target = 1, unit(half, wrap(first + 2), 0, 2), through.at[half, 0]
         elif move == 3:
-            way, source, target = -1, unit(part, half, wrap(first + 2), 2, 2), through.at[half, 1]
+            way, source, target = -1, unit(half, wrap(first + 2), 2, 2), through.at[half, 1]
         elif move == 4:
             way, source, target = 1, through.at[half, 0], close.at[half, 2, pl.ds(0, 2)]
         elif move == 5:
             way, source, target = -1, through.at[half, 1], close.at[half, 2, pl.ds(2, 2)]
         else:
             way = (1, -1, 2)[move - 6]
-            source = summed[part].at[half, wrap(second + way)]
-            target = last[part].at[half, move - 6]
+            source = summed.at[half, wrap(second + way)]
+            target = last.at[half, move - 6]
         if move < 6:
             peer = place(half, wrap(first + way), second)
         else:
@@ -370,114 +342,91 @@
         return pltpu.make_async_remote_copy(
             src_ref=source,
             dst_ref=target,
-            send_sem=sum_send.at[part, half, move],
-            recv_sem=sum_recv.at[part, half, move],
+            send_sem=sum_send.at[half, move],
+            recv_sem=sum_recv.at[half, move],
             device_id={"dp": peer},
             device_id_type=MESH,
         )
 
-    def tally_relay(part):
+    def tally_relay():
         for half in halves:
-            tally(part, half, 2).wait_recv()
-            tally(part, half, 4).start()
-            tally(part, half, 3).wait_recv()
-            tally(part, half, 5).start()
-
-    def tally_near(part):
+            tally(half, 2).wait_recv()
+            tally(half, 4).start()
+            tally(half, 3).wait_recv()
+            tally(half, 5).start()
+
+    def tally_near():
         for half in halves:
             for move in (0, 1, 4, 5):
-                tally(part, half, move).wait_recv()
+                tally(half, move).wait_recv()
             index = spot_x if half == 0 else spot_y
             rows = slice(half * HALF, half * HALF + HALF)
             for spot in range(SIDE):
                 if half == 0:
-                    own = parts[part][index, spot, rows, :]
+                    own = parts[index, spot, rows, :]
                 else:
-                    own = parts[part][spot, index, rows, :]
+                    own = parts[spot, index, rows, :]
                 value = own.astype(F32)
                 for source in range(3):
-                    value = value + near[part][half, source, spot].astype(F32)
-                summed[part][half, spot] = value.astype(BF16)
+                    value = value + near[half, source, spot].astype(F32)
+                summed[half, spot] = value.astype(BF16)
             for move in (8, 6, 7):
-                tally(part, half, move).start()
-
-    def give_back(part):
+                tally(half, move).start()
+
+    def give_back():
         totals = []
         for half in halves:
             for move in (6, 7, 8):
-                tally(part, half, move).wait_recv()
+                tally(half, move).wait_recv()
             index = spot_y if half == 0 else spot_x
-            value = summed[part][half, index].astype(F32)
+            value = summed[half, index].astype(F32)
             for source in range(3):
-                value = value + last[part][half, source].astype(F32)
+                value = value + last[half, source].astype(F32)
             totals.append(value.astype(BF16))
         total = jnp.concatenate(totals, axis=0)
-        send[3 + part][...] = turned(slot_hits, total).astype(BF16).reshape(send[3 + part].shape)
-        cross_start(3 + part)
+        send[2][...] = turned(slot_hits, total).astype(BF16).reshape(send[2].shape)
+        cross_start(2)
 
     backward(wrap(spot_x + 2))
-    project(0, wrap(spot_x + 2))
-    tally(0, 0, 2).start()
-    tally(0, 0, 3).start()
+    tally(0, 2).start()
+    tally(0, 3).start()
     backward(wrap(spot_x + 1))
-    project(0, wrap(spot_x + 1))
-    tally(0, 0, 0).start()
+    tally(0, 0).start()
     backward(wrap(spot_x - 1))
-    project(0, wrap(spot_x - 1))
-    tally(0, 0, 1).start()
+    tally(0, 1).start()
     backward(spot_x)
-    project(0, spot_x)
     for move in (2, 3, 0, 1):
-        tally(0, 1, move).start()
-    for chunk in range(SIDE):
-        project(1, chunk)
-    tally_relay(0)
-    for move in (2, 3, 0, 1):
-        for half in halves:
-            tally(1, half, move).start()
+        tally(1, move).start()
+    tally_relay()
     hidden_rows = hidden[...].reshape(SIDE * hidden.shape[1], hidden.shape[2])
     grad_rows = grad_pre[...].reshape(hidden_rows.shape)
 
-    def weight_out(which):
-        begin, count = spans[which]
-        rows = full[which][...].reshape(hidden_rows.shape[0], count)
-        hold_wout[:, begin : begin + count] = turned(hidden_rows, rows).astype(BF16)
-
-    def weight_in(begin, count):
-        rows = full[0][:, :, begin : begin + count].reshape(hidden_rows.shape[0], count)
-        hold_win[begin : begin + count, :] = turned(rows, grad_rows).astype(BF16)
-
-    weight_out(1)
-    tally_near(0)
-    tally_relay(1)
-    give_back(0)
-    tally_near(1)
-    weight_out(2)
-    give_back(1)
+    rows_grad = full[1][...].reshape(hidden_rows.shape[0], width)
+    hold_wout[...] = turned(hidden_rows, rows_grad).astype(BF16)
     store_wout = pltpu.make_async_copy(hold_wout, out_wout, load_sem.at[4])
     store_wout.start()
-    weight_in(*spans[1])
-    weight_in(*spans[2])
+    tally_near()
+    give_back()
+    for begin, count in ((0, CUT), (CUT, width - CUT)):
+        rows_in = full[0][:, :, begin : begin + count].reshape(hidden_rows.shape[0], count)
+        hold_win[begin : begin + count, :] = turned(rows_in, grad_rows).astype(BF16)
     store_win = pltpu.make_async_copy(hold_win, out_win, load_sem.at[5])
     store_win.start()
-    for which in range(3):
+    for which in range(2):
         spread_sent(which)
-    for part in range(2):
-        for half in halves:
-            for move in range(9):
-                tally(part, half, move).wait_send()
-    for i in range(3):
-        cross_sent(i)
-    cross_wait(3)
-    cross_wait(4)
-    cross_sent(3)
-    cross_sent(4)
+    for half in halves:
+        for move in range(9):
+            tally(half, move).wait_send()
+    cross_sent(0)
+    cross_sent(1)
+    cross_wait(2)
+    cross_sent(2)
     store_wout.wait()
     store_win.wait()
 
 
 def tail_kernel(
-    picks, back_a, back_b, win_hbm, wout_hbm, out_patches, out_win, out_wout, win, wout, sem_in, sem_out
+    picks, back, win_hbm, wout_hbm, out_patches, out_win, out_wout, win, wout, sem_in, sem_out
 ):
     width = out_patches.shape[1]
     loads, stores = [], []
@@ -491,11 +440,8 @@
     for load in loads:
         load.start()
     owner_hits = pick_table(picks, out_patches.shape[0])
-    for (begin, count), back in zip(widths_of(width)[1:], (back_a, back_b)):
-        rows = back[...].reshape(back.shape[0] * back.shape[1], count)
-        out_patches[:, begin : begin + count] = jnp.dot(
-            owner_hits, rows, preferred_element_type=F32
-        ).astype(BF16)
+    rows = back[...].reshape(back.shape[0] * back.shape[1], width)
+    out_patches[...] = jnp.dot(owner_hits, rows, preferred_element_type=F32).astype(BF16)
     for load, store in zip(loads, stores):
         load.wait()
         store.start()
@@ -512,19 +458,17 @@
     capacity = gates.shape[2]
     units = weight_in.shape[2]
     side_rows = groups * capacity // SIDE
-    parts = [count for _, count in widths_of(width)]
     in_vmem = pl.BlockSpec(memory_space=pltpu.VMEM)
     in_place = pl.BlockSpec(memory_space=pl.ANY)
     shape_in = jax.ShapeDtypeStruct((width, units), BF16)
     shape_out = jax.ShapeDtypeStruct((units, width), BF16)
     local_picks = jnp.transpose(picks[0, 0])
-    slabs = [pltpu.VMEM((experts, ranks, count), BF16) for count in parts + parts[1:]]
-    back_a, back_b, grad_in, grad_out_weight = pl.pallas_call(
+    slab = (experts, ranks, width)
+    back, grad_in, grad_out_weight = pl.pallas_call(
         layer_kernel,
-        out_shape=[jax.ShapeDtypeStruct((experts, ranks, count), BF16) for count in parts[1:]]
-        + [shape_in, shape_out],
+        out_shape=[jax.ShapeDtypeStruct(slab, BF16), shape_in, shape_out],
         in_specs=[in_place] * 4 + [in_vmem] * 3,
-        out_specs=[in_vmem] * 2 + [in_place] * 2,
+        out_specs=[in_vmem] + [in_place] * 2,
         scratch_shapes=[
             pltpu.VMEM((tokens, width), BF16),
             pltpu.VMEM((tokens, width), BF16),
@@ -533,30 +477,26 @@
             pltpu.VMEM((width, units), BF16),
             pltpu.VMEM((units, width), BF16),
         ]
-        + slabs
-        + slabs[:3]
-        + [pltpu.VMEM((capacity, count), BF16) for count in parts]
-        + [pltpu.VMEM((groups, capacity, count), BF16) for count in parts]
+        + [pltpu.VMEM(slab, BF16)] * 5
+        + [pltpu.VMEM((capacity, width), BF16)] * 2
+        + [pltpu.VMEM((groups, capacity, width), BF16)] * 2
         + [
             pltpu.VMEM((SIDE, side_rows, units), BF16),
             pltpu.VMEM((SIDE, side_rows, units), F32),
-            pltpu.VMEM((SIDE, side_rows, units), F32),
             pltpu.VMEM((SIDE, side_rows, units), BF16),
-        ]
-        + [pltpu.VMEM((SIDE, SIDE, capacity, count), BF16) for count in parts[1:]]
-        + [pltpu.VMEM((2, 3, SIDE, HALF, count), BF16) for count in parts[1:]]
-        + [pltpu.VMEM((2, 2, 2, HALF, count), BF16) for count in parts[1:]]
-        + [pltpu.VMEM((2, SIDE, HALF, count), BF16) for count in parts[1:]]
-        + [pltpu.VMEM((2, 3, HALF, count), BF16) for count in parts[1:]]
-        + [
+            pltpu.VMEM((SIDE, SIDE, capacity, width), BF16),
+            pltpu.VMEM((2, 3, SIDE, HALF, width), BF16),
+            pltpu.VMEM((2, 2, 2, HALF, width), BF16),
+            pltpu.VMEM((2, SIDE, HALF, width), BF16),
+            pltpu.VMEM((2, 3, HALF, width), BF16),
             pltpu.SemaphoreType.DMA((6,)),
-            pltpu.SemaphoreType.DMA((8,)),
-            pltpu.SemaphoreType.DMA((5, experts)),
-            pltpu.SemaphoreType.DMA((5, experts)),
-            pltpu.SemaphoreType.DMA((3, 2, 5, 4)),
-            pltpu.SemaphoreType.DMA((3, 2, 5, 4)),
-            pltpu.SemaphoreType.DMA((2, 2, 9)),
-            pltpu.SemaphoreType.DMA((2, 2, 9)),
+            pltpu.SemaphoreType.DMA((5,)),
+            pltpu.SemaphoreType.DMA((3, experts)),
+            pltpu.SemaphoreType.DMA((3, experts)),
+            pltpu.SemaphoreType.DMA((2, 2, 5, 4)),
+            pltpu.SemaphoreType.DMA((2, 2, 5, 4)),
+            pltpu.SemaphoreType.DMA((2, 9)),
+            pltpu.SemaphoreType.DMA((2, 9)),
         ],
         compiler_params=pltpu.CompilerParams(
             collective_id=1, has_side_effects=True, vmem_limit_bytes=56 * 1024 * 1024
@@ -573,7 +513,7 @@
     grad_patches, grad_in, grad_out_weight = pl.pallas_call(
         tail_kernel,
         out_shape=[jax.ShapeDtypeStruct((tokens, width), BF16), shape_in, shape_out],
-        in_specs=[in_vmem] * 3 + [in_place] * 2,
+        in_specs=[in_vmem] * 2 + [in_place] * 2,
         out_specs=[in_vmem] + [in_place] * 2,
         scratch_shapes=[
             pltpu.VMEM((width, units), BF16),
@@ -582,7 +522,7 @@
             pltpu.SemaphoreType.DMA((4,)),
         ],
         compiler_params=pltpu.CompilerParams(vmem_limit_bytes=56 * 1024 * 1024),
-    )(local_picks, back_a, back_b, grad_in, grad_out_weight)
+    )(local_picks, back, grad_in, grad_out_weight)
     return (grad_patches[None, None], grad_in[None], grad_out_weight[None])
 
 

time: 115 us -> 96.1 us (0.84)
  Pallas kernels: 114 us -> 95.2 us
    pallas_call x1, Pallas kernels: 110 us -> 91.2 us  [on_device(): pl.pallas_call(layer_kernel, out_shape=[jax.ShapeDtypeStruct(slab, BF16),...]
where the time goes in v4:
time: 96.1 us; the launch traced here: 95.8 us
  Pallas kernels  95.2 us (99%)
    pallas_call x1, Pallas kernels, on_device(): pl.pallas_call(layer_kernel, out_shape=[jax.ShapeDtypeStruct(slab, BF16),...  91.2 us
    pallas_call x1, Pallas kernels, on_device(): pl.pallas_call(tail_kernel, out_shape=[jax.ShapeDtypeStruct((tokens, widt...  3.96 us

profile of v4, /device:TPU:1, one launch (start us, length us, event | category | flops | bytes accessed | tf_op | source)
XLA Modules:
  0.0 95.8 jit_solution(9799767289768071818)
XLA Ops:
  0.6 91.2 %shard_map.94 = (bf16[32,2,1664]{2,1,0:T(2,128)(2,1)}, bf16[1664,256]{1,0:T(8,128)(2,1)}, bf16[256,1664]{1,0:T(8,128)(2,1)}) custom-call(bf16[128,1664]{1,0:T(8,128)(2,1)} %bitcast.14, bf16[128,1664]{1,0:T(8,128)(2,1)} %bitcast.15, bf16[1664,256]{1,0:T(8,128)(2,1)} %bitcast.12, bf16[256,1664]{1,0:T(8,128)(2,1)} %bitcast.13, f32[1,32]{1,0:T(1,128)} %bitcast.19, ...), custom_call_target="tpu_custom_call" | custom-call | tf_op jit(solution)/shard_map/pallas_call | solution.py:467
  91.9 4.0 %shard_map.95 = (bf16[128,1664]{1,0:T(8,128)(2,1)}, bf16[1664,256]{1,0:T(8,128)(2,1)}, bf16[256,1664]{1,0:T(8,128)(2,1)}) custom-call(s32[2,32]{1,0:T(2,128)} %bitcast.18, bf16[32,2,1664]{2,1,0:T(2,128)(2,1)} %get-tuple-element.9.back, bf16[1664,256]{1,0:T(8,128)(2,1)} %get-tuple-element.10.win_hbm, bf16[256,1664]{1,0:T(8,128)(2,1)} %get-tuple-element.11.wout_hbm), custom_call_target="tpu_custom_call" | custom-call | tf_op jit(solution)/shard_map/pallas_call | solution.py:513

commit v5 on v4

--- a/solution.py
+++ b/solution.py
@@ -298,13 +298,13 @@
     mine[1][...] = (gate_col * compact(1)).astype(BF16)
     spread_one(1)
     spread_four(0)
+    spread_two(1)
     spread_five(0)
-    spread_two(1)
     loads[2].wait()
+    spread_three(1)
     forward(0)
-    spread_three(1)
+    spread_four(1)
     forward(1)
-    spread_four(1)
     forward(2)
     forward(3)
     spread_five(1)

time: 96.1 us -> 94.2 us (0.980)
  Pallas kernels: 95.2 us -> 93.3 us
    pallas_call x1, Pallas kernels: 91.2 us -> 89.4 us  [on_device(): pl.pallas_call(layer_kernel, out_shape=[jax.ShapeDtypeStruct(slab, BF16),...]
where the time goes in v5:
time: 94.2 us; the launch traced here: 94 us
  Pallas kernels  93.3 us (99%)
    pallas_call x1, Pallas kernels, on_device(): pl.pallas_call(layer_kernel, out_shape=[jax.ShapeDtypeStruct(slab, BF16),...  89.4 us
    pallas_call x1, Pallas kernels, on_device(): pl.pallas_call(tail_kernel, out_shape=[jax.ShapeDtypeStruct((tokens, widt...  3.96 us

profile of v5, /device:TPU:1, one launch (start us, length us, event | category | flops | bytes accessed | tf_op | source)
XLA Modules:
  0.0 94.0 jit_solution(12982130168366275052)
XLA Ops:
  0.6 89.4 %shard_map.94 = (bf16[32,2,1664]{2,1,0:T(2,128)(2,1)}, bf16[1664,256]{1,0:T(8,128)(2,1)}, bf16[256,1664]{1,0:T(8,128)(2,1)}) custom-call(bf16[128,1664]{1,0:T(8,128)(2,1)} %bitcast.14, bf16[128,1664]{1,0:T(8,128)(2,1)} %bitcast.15, bf16[1664,256]{1,0:T(8,128)(2,1)} %bitcast.12, bf16[256,1664]{1,0:T(8,128)(2,1)} %bitcast.13, f32[1,32]{1,0:T(1,128)} %bitcast.19, ...), custom_call_target="tpu_custom_call" | custom-call | tf_op jit(solution)/shard_map/pallas_call | solution.py:467
  90.0 4.0 %shard_map.95 = (bf16[128,1664]{1,0:T(8,128)(2,1)}, bf16[1664,256]{1,0:T(8,128)(2,1)}, bf16[256,1664]{1,0:T(8,128)(2,1)}) custom-call(s32[2,32]{1,0:T(2,128)} %bitcast.18, bf16[32,2,1664]{2,1,0:T(2,128)(2,1)} %get-tuple-element.9.back, bf16[1664,256]{1,0:T(8,128)(2,1)} %get-tuple-element.10.win_hbm, bf16[256,1664]{1,0:T(8,128)(2,1)} %get-tuple-element.11.wout_hbm), custom_call_target="tpu_custom_call" | custom-call | tf_op jit(solution)/shard_map/pallas_call | solution.py:513
